TPU v7x, 32 devices: a whole 2x2x4 slice. The times are simulated.
32 devices in a mesh: dp: 4 (over y, core), seq: 4 (over z), tensor: 2 (over x).
Axes of the slice: x: 2, y: 2, z: 4, core: 2. Of those that a mesh axis runs over, the one named last changes fastest.
Arguments:
- tokens: bfloat16 [8192, 2048], P(('dp', 'seq')), may hold values from -6 to 6
- out_grad: bfloat16 [8192, 2048], P(('dp', 'seq')), may hold values from -6 to 6
- positions: int32 [4, 2048], P('dp'), may hold values from 0 to 1151, as said below
- attn_gain: float32 [2048], P(('dp', 'seq')), may hold values from 0.5 to 1.5
- q_weight: float32 [2048, 2048], P(('dp', 'seq'), 'tensor'), may hold values from -0.125 to 0.125
- k_weight: float32 [2048, 512], P(('dp', 'seq'), 'tensor'), may hold values from -0.125 to 0.125
- v_weight: float32 [2048, 512], P(('dp', 'seq'), 'tensor'), may hold values from -0.125 to 0.125
- o_weight: float32 [2048, 2048], P(('dp', 'seq'), 'tensor'), may hold values from -1.5 to 1.5
- mlp_gain: float32 [2048], P(('dp', 'seq')), may hold values from 0.5 to 1.5
- gate_weight: float32 [2048, 8192], P(('dp', 'seq'), 'tensor'), may hold values from -0.125 to 0.125
- up_weight: float32 [2048, 8192], P(('dp', 'seq'), 'tensor'), may hold values from -0.125 to 0.125
- down_weight: float32 [2048, 8192], P(('dp', 'seq'), 'tensor'), may hold values from -0.0625 to 0.0625
Outputs:
- output: bfloat16 [8192, 2048], P(('dp', 'seq'))
- tokens_grad: bfloat16 [8192, 2048], P(('dp', 'seq'))
- attn_gain_grad: float32 [2048], P(('dp', 'seq'))
- q_weight_grad: float32 [2048, 2048], P(('dp', 'seq'), 'tensor')
- k_weight_grad: float32 [2048, 512], P(('dp', 'seq'), 'tensor')
- v_weight_grad: float32 [2048, 512], P(('dp', 'seq'), 'tensor')
- o_weight_grad: float32 [2048, 2048], P(('dp', 'seq'), 'tensor')
- mlp_gain_grad: float32 [2048], P(('dp', 'seq'))
- gate_weight_grad: float32 [2048, 8192], P(('dp', 'seq'), 'tensor')
- up_weight_grad: float32 [2048, 8192], P(('dp', 'seq'), 'tensor')
- down_weight_grad: float32 [2048, 8192], P(('dp', 'seq'), 'tensor')
Inputs may be any that keep to these rules, and one draw needn't show every extreme that they name: In each group, every block of 512 rows (aligned) holds 256 prompt tokens followed by 2 whole continuations of 128 rows; the prompt's positions 0 to 1023 each occur once in the group, in a drawn order; a continuation's rows hold positions 1024 to 1151 in order.
All inputs are finite; a program needn't handle non-finite values.
Results may differ from a plain program's by a relative error of at most 0.018.
Values may be sent and summed in bfloat16 or wider, within the bound.
A program may use at most 384 MiB of HBM per device.

v0:
```python
import math

import jax
import jax.numpy as jnp
import numpy as np
from jax import lax
from jax.sharding import PartitionSpec as P

HEAD_DIM = 64
PROMPT = 1024
CONT_LEN = 128


epsilon = 1e-05


def for_sending(array):
    return jax.tree.map(lambda a: a.astype(jnp.bfloat16) if a.dtype == jnp.float32 else a, array)


def rope_freqs(head_width):
    scaled_list = []
    for column in range(head_width // 2):
        inverse = 1.0 / 500000.0 ** (2.0 * column / head_width)
        wavelength = 2.0 * math.pi / inverse
        if wavelength < 2048.0:
            scaled_list.append(inverse)
        elif wavelength > 8192.0:
            scaled_list.append(inverse / 32.0)
        else:
            smooth_mix = (8192.0 / wavelength - 1.0) / 3.0
            scaled_list.append((1.0 - smooth_mix) * inverse / 32.0 + smooth_mix * inverse)
    return np.array(scaled_list, dtype=np.float32)


def rope_apply(values, cos_table, sin_table):
    half_width = values.shape[-1] // 2
    turned = jnp.concatenate([-values[..., half_width:], values[..., :half_width]], axis=-1)
    return values * cos_table + turned * sin_table


def rope_back(grads, cos_table, sin_table):
    half_width = grads.shape[-1] // 2
    twisted = grads * sin_table
    return grads * cos_table + jnp.concatenate(
        [twisted[..., half_width:], -twisted[..., :half_width]], axis=-1
    )


def norm_parts(values):
    inv_rms = lax.rsqrt(jnp.mean(values * values, axis=-1, keepdims=True) + epsilon)
    return (values * inv_rms, inv_rms)


def norm_back(grad_normed, unit_rows, inv_rms, gain_vec):
    grad_unit = grad_normed * gain_vec
    return inv_rms * (
        grad_unit - unit_rows * jnp.mean(grad_unit * unit_rows, axis=-1, keepdims=True)
    )


def times_transposed(left_side, right_side):
    return lax.dot_general(
        left_side, right_side, (((1,), (1,)), ((), ())), preferred_element_type=jnp.float32
    )


def transposed_times(left_side, right_side):
    return lax.dot_general(
        left_side, right_side, (((0,), (0,)), ((), ())), preferred_element_type=jnp.float32
    )


def local(
    tokens,
    out_grad,
    positions,
    attn_gain,
    q_weight,
    k_weight,
    v_weight,
    o_weight,
    mlp_gain,
    gate_weight,
    up_weight,
    down_weight,
):
    seq_count = lax.axis_size("seq")
    seq_rank = lax.axis_index("seq")
    tok_rows = tokens.shape[0]
    prompt_rows = PROMPT // seq_count
    cont_here = (tok_rows - prompt_rows) // CONT_LEN
    all_pos = positions[0]
    own_pos = lax.dynamic_slice_in_dim(all_pos, seq_rank * tok_rows, tok_rows)
    row_offset = jnp.arange(tok_rows, dtype=jnp.int32)
    cont_number = 1 + seq_rank * cont_here + (row_offset - prompt_rows) // CONT_LEN
    own_seg = jnp.where(row_offset < prompt_rows, jnp.zeros_like(row_offset), cont_number)
    prompt_pos = all_pos.reshape(seq_count, tok_rows)[:, :prompt_rows].reshape(-1)
    key_pos = jnp.concatenate([prompt_pos, own_pos[prompt_rows:]])
    key_seg = jnp.concatenate([jnp.zeros_like(prompt_pos), own_seg[prompt_rows:]])
    visible = (key_pos[None, :] <= own_pos[:, None]) & (
        (key_seg[None, :] == 0) | (key_seg[None, :] == own_seg[:, None])
    )
    prompt_count = prompt_pos.shape[0]
    angles = (
        own_pos.astype(jnp.float32)[:, None]
        * jnp.asarray(rope_freqs(HEAD_DIM), jnp.float32)[None, :]
    )
    angles = jnp.concatenate([angles, angles], axis=1)
    cos_table = jnp.cos(angles)[:, None, :]
    sin_table = jnp.sin(angles)[:, None, :]
    score_scale = 1.0 / math.sqrt(HEAD_DIM)

    def attn_pack():
        return (
            attn_gain.astype(jnp.bfloat16),
            q_weight.astype(jnp.bfloat16),
            k_weight.astype(jnp.bfloat16),
            v_weight.astype(jnp.bfloat16),
            o_weight.astype(jnp.bfloat16),
        )

    def mlp_pack():
        return (
            mlp_gain.astype(jnp.bfloat16),
            gate_weight.astype(jnp.bfloat16),
            up_weight.astype(jnp.bfloat16),
            down_weight.astype(jnp.bfloat16),
        )

    attn_set = lax.all_gather(for_sending(attn_pack()), ("dp", "seq"), axis=0, tiled=True)
    mlp_set = lax.all_gather(for_sending(mlp_pack()), ("dp", "seq"), axis=0, tiled=True)
    inputs = tokens.astype(jnp.float32)
    unit_one, rms_one = norm_parts(inputs)
    normed = (unit_one * attn_set[0].astype(jnp.float32)).astype(jnp.bfloat16)
    query_raw = jnp.dot(normed, attn_set[1], preferred_element_type=jnp.float32)
    key_raw = jnp.dot(normed, attn_set[2], preferred_element_type=jnp.float32)
    value_raw = jnp.dot(normed, attn_set[3], preferred_element_type=jnp.float32)
    local_heads = query_raw.shape[1] // HEAD_DIM
    local_kv = key_raw.shape[1] // HEAD_DIM
    group_size = local_heads // local_kv
    queries = rope_apply(
        query_raw.reshape(tok_rows, local_heads, HEAD_DIM), cos_table, sin_table
    ).astype(jnp.bfloat16)
    keys_own = (
        rope_apply(key_raw.reshape(tok_rows, local_kv, HEAD_DIM), cos_table, sin_table)
        .astype(jnp.bfloat16)
        .reshape(tok_rows, -1)
    )
    values_own = value_raw.astype(jnp.bfloat16)
    prompt_keys, prompt_values = (
        lax.all_gather(keys_own[:prompt_rows], "seq", axis=0, tiled=True),
        lax.all_gather(values_own[:prompt_rows], "seq", axis=0, tiled=True),
    )
    key_all = jnp.concatenate([prompt_keys, keys_own[prompt_rows:]], axis=0).reshape(
        -1, local_kv, HEAD_DIM
    )
    value_all = jnp.concatenate([prompt_values, values_own[prompt_rows:]], axis=0).reshape(
        -1, local_kv, HEAD_DIM
    )

    def head_scores(query_group, key_group):
        scores = (
            jnp.einsum("tgd,cd->gtc", query_group, key_group, preferred_element_type=jnp.float32)
            * score_scale
        )
        return jnp.where(visible[None], scores, -1e30)

    mixed_list = []
    log_totals = []
    for kv_head in range(local_kv):
        query_group = queries[:, kv_head * group_size : (kv_head + 1) * group_size, :]
        scores = head_scores(query_group, key_all[:, kv_head, :])
        row_max = jnp.max(scores, axis=-1, keepdims=True)
        exponent = jnp.exp(scores - row_max)
        row_total = jnp.sum(exponent, axis=-1, keepdims=True)
        probability = exponent / row_total
        log_totals.append(row_max + jnp.log(row_total))
        mixed_list.append(
            jnp.einsum(
                "gtc,cd->tgd",
                probability.astype(jnp.bfloat16),
                value_all[:, kv_head, :],
                preferred_element_type=jnp.float32,
            )
        )
    attended = jnp.concatenate(mixed_list, axis=1).reshape(tok_rows, -1).astype(jnp.bfloat16)
    middle = inputs + lax.psum(
        times_transposed(attended, attn_set[4]).astype(jnp.bfloat16), "tensor"
    ).astype(jnp.float32)
    unit_two, rms_two = norm_parts(middle)
    normed_two = (unit_two * mlp_set[0].astype(jnp.float32)).astype(jnp.bfloat16)
    gate_pre = jnp.dot(normed_two, mlp_set[1], preferred_element_type=jnp.float32)
    upward = jnp.dot(normed_two, mlp_set[2], preferred_element_type=jnp.float32)
    sigmoid_gate = jax.nn.sigmoid(gate_pre)
    activated = gate_pre * sigmoid_gate
    hidden = (activated * upward).astype(jnp.bfloat16)
    result = middle + lax.psum(
        times_transposed(hidden, mlp_set[3]).astype(jnp.bfloat16), "tensor"
    ).astype(jnp.float32)
    output = result.astype(jnp.bfloat16)
    attn_set = lax.all_gather(for_sending(attn_pack()), ("dp", "seq"), axis=0, tiled=True)
    mlp_set = lax.all_gather(for_sending(mlp_pack()), ("dp", "seq"), axis=0, tiled=True)
    grad_out = out_grad.astype(jnp.float32)
    grad_hidden = jnp.dot(out_grad, mlp_set[3], preferred_element_type=jnp.float32)
    grad_gate = (
        grad_hidden * upward * sigmoid_gate * (1.0 + gate_pre * (1.0 - sigmoid_gate))
    ).astype(jnp.bfloat16)
    grad_up = (grad_hidden * activated).astype(jnp.bfloat16)
    grad_normed_two = lax.psum(
        (times_transposed(grad_gate, mlp_set[1]) + times_transposed(grad_up, mlp_set[2])).astype(
            jnp.bfloat16
        ),
        "tensor",
    ).astype(jnp.float32)
    gain_two_grad = jnp.sum(grad_normed_two * unit_two, axis=0)
    grad_middle = grad_out + norm_back(
        grad_normed_two, unit_two, rms_two, mlp_set[0].astype(jnp.float32)
    )
    mlp_grads = lax.psum_scatter(
        jnp.concatenate(
            [
                transposed_times(normed_two, grad_gate),
                transposed_times(normed_two, grad_up),
                transposed_times(out_grad, hidden),
            ],
            axis=1,
        ),
        ("dp", "seq"),
        scatter_dimension=0,
        tiled=True,
    )
    ff_local = gate_weight.shape[1]
    grad_branch = grad_middle.astype(jnp.bfloat16)
    grad_attended = (
        jnp.dot(grad_branch, attn_set[4], preferred_element_type=jnp.float32)
        .astype(jnp.bfloat16)
        .reshape(tok_rows, local_heads, HEAD_DIM)
    )
    query_grads = []
    key_grads = []
    value_grads = []
    for kv_head in range(local_kv):
        query_group = queries[:, kv_head * group_size : (kv_head + 1) * group_size, :]
        key_group = key_all[:, kv_head, :]
        value_group = value_all[:, kv_head, :]
        grad_group = grad_attended[:, kv_head * group_size : (kv_head + 1) * group_size, :]
        probability = jnp.exp(head_scores(query_group, key_group) - log_totals[kv_head])
        grad_prob = jnp.einsum(
            "tgd,cd->gtc", grad_group, value_group, preferred_element_type=jnp.float32
        )
        row_dot = jnp.sum(probability * grad_prob, axis=-1, keepdims=True)
        grad_scores = (probability * (grad_prob - row_dot)).astype(jnp.bfloat16)
        query_grads.append(
            jnp.einsum("gtc,cd->tgd", grad_scores, key_group, preferred_element_type=jnp.float32)
            * score_scale
        )
        key_grads.append(
            jnp.einsum("gtc,tgd->cd", grad_scores, query_group, preferred_element_type=jnp.float32)
            * score_scale
        )
        value_grads.append(
            jnp.einsum(
                "gtc,tgd->cd",
                probability.astype(jnp.bfloat16),
                grad_group,
                preferred_element_type=jnp.float32,
            )
        )
    grad_queries = jnp.concatenate(query_grads, axis=1)
    grad_keys = jnp.stack(key_grads, axis=1).reshape(-1, local_kv * HEAD_DIM)
    grad_values = jnp.stack(value_grads, axis=1).reshape(-1, local_kv * HEAD_DIM)
    key_share, value_share = (
        lax.psum_scatter(
            grad_keys[:prompt_count].astype(jnp.bfloat16), "seq", scatter_dimension=0, tiled=True
        ).astype(jnp.float32),
        lax.psum_scatter(
            grad_values[:prompt_count].astype(jnp.bfloat16), "seq", scatter_dimension=0, tiled=True
        ).astype(jnp.float32),
    )
    grad_key_own = jnp.concatenate([key_share, grad_keys[prompt_count:]], axis=0).reshape(
        tok_rows, local_kv, HEAD_DIM
    )
    grad_query_raw = (
        rope_back(grad_queries, cos_table, sin_table).reshape(tok_rows, -1).astype(jnp.bfloat16)
    )
    grad_key_raw = (
        rope_back(grad_key_own, cos_table, sin_table).reshape(tok_rows, -1).astype(jnp.bfloat16)
    )
    grad_value_raw = jnp.concatenate([value_share, grad_values[prompt_count:]], axis=0).astype(
        jnp.bfloat16
    )
    grad_normed = lax.psum(
        (
            times_transposed(grad_query_raw, attn_set[1])
            + times_transposed(grad_key_raw, attn_set[2])
            + times_transposed(grad_value_raw, attn_set[3])
        ).astype(jnp.bfloat16),
        "tensor",
    ).astype(jnp.float32)
    gain_one_grad = jnp.sum(grad_normed * unit_one, axis=0)
    grad_inputs = grad_middle + norm_back(
        grad_normed, unit_one, rms_one, attn_set[0].astype(jnp.float32)
    )
    attn_terms = (
        gain_one_grad,
        transposed_times(normed, grad_query_raw),
        transposed_times(normed, grad_key_raw),
        transposed_times(normed, grad_value_raw),
        transposed_times(grad_branch, attended),
        gain_two_grad,
    )
    attn_grads = (
        lax.psum_scatter(attn_terms[0], ("dp", "seq"), scatter_dimension=0, tiled=True),
        lax.psum_scatter(attn_terms[1], ("dp", "seq"), scatter_dimension=0, tiled=True),
        lax.psum_scatter(attn_terms[2], ("dp", "seq"), scatter_dimension=0, tiled=True),
        lax.psum_scatter(attn_terms[3], ("dp", "seq"), scatter_dimension=0, tiled=True),
        lax.psum_scatter(attn_terms[4], ("dp", "seq"), scatter_dimension=0, tiled=True),
        lax.psum_scatter(attn_terms[5], ("dp", "seq"), scatter_dimension=0, tiled=True),
    )
    return (
        output,
        grad_inputs.astype(jnp.bfloat16),
        attn_grads[0],
        attn_grads[1],
        attn_grads[2],
        attn_grads[3],
        attn_grads[4],
        attn_grads[5],
        mlp_grads[:, :ff_local],
        mlp_grads[:, ff_local : 2 * ff_local],
        mlp_grads[:, 2 * ff_local :],
    )


def solution(mesh):
    placed = (
        P(("dp", "seq"), None),
        P(("dp", "seq"), None),
        P("dp", None),
        P(("dp", "seq")),
        P(("dp", "seq"), "tensor"),
        P(("dp", "seq"), "tensor"),
        P(("dp", "seq"), "tensor"),
        P(("dp", "seq"), "tensor"),
        P(("dp", "seq")),
        P(("dp", "seq"), "tensor"),
        P(("dp", "seq"), "tensor"),
        P(("dp", "seq"), "tensor"),
    )
    return jax.shard_map(
        local,
        mesh=mesh,
        in_specs=placed,
        out_specs=(
            P(("dp", "seq"), None),
            P(("dp", "seq"), None),
            P(("dp", "seq")),
            P(("dp", "seq"), "tensor"),
            P(("dp", "seq"), "tensor"),
            P(("dp", "seq"), "tensor"),
            P(("dp", "seq"), "tensor"),
            P(("dp", "seq")),
            P(("dp", "seq"), "tensor"),
            P(("dp", "seq"), "tensor"),
            P(("dp", "seq"), "tensor"),
        ),
        check_vma=False,
    )
```

profile of v0, /device:TPU:0, one launch (start us, length us, event | category | flops | bytes accessed | tf_op | source)
XLA Modules:
  0.0 3029.8 jit_solution(11983478142990377028)
XLA Ops:
  15.0 33.9 %all-gather = bf16[16,1,128]{2,1,0:T(2,128)(2,1)S(1)} all-gather(bf16[1,1,128]{2,1,0:T(2,128)(2,1)S(1)} %convert_bitcast_fusion.1), channel_id=1, replica_groups=mesh['dp'=4,'seq'=4,'tensor'=2] {'dp','seq'}, dimensions={0}, use_global_device_ids=true | all-gather | bytes 4352 | tf_op jit(solution)/shard_map/all_gather | solution.py:131
  56.4 16.3 all_gather.46
  72.7 18.9 all-gather.10.cloned.1.call-done
  93.7 19.2 all_gather.44
  116.6 29.1 all-gather.14.cloned.1.call-done
  212.6 30.1 all-gather.1
  245.1 19.8 all-reduce.11.cloned.1.call-done
  270.3 123.6 %all-gather.18.cloned.1.call-done = bf16[2048,4096]{1,0:T(8,128)(2,1)} async-done(((bf16[128,4096]{1,0:T(8,128)(2,1)}), bf16[2048,4096]{1,0:T(8,128)(2,1)}) %all-gather.18.cloned.1.call-update) | async-done | bytes 16777232 | tf_op jit(solution)/shard_map/all_gather | solution.py:132
  408.9 112.5 %all-gather.20.cloned.1.call-done = bf16[2048,4096]{1,0:T(8,128)(2,1)} async-done(((bf16[128,4096]{1,0:T(8,128)(2,1)}), bf16[2048,4096]{1,0:T(8,128)(2,1)}) %all-gather.20.cloned.1.call-update) | async-done | bytes 16777232 | tf_op jit(solution)/shard_map/all_gather | solution.py:132
  521.4 14.9 fusion.164
  536.3 112.5 %all-gather.22.cloned.1.call-done = bf16[2048,4096]{1,0:T(8,128)(2,1)} async-done(((bf16[128,4096]{1,0:T(8,128)(2,1)}), bf16[2048,4096]{1,0:T(8,128)(2,1)}) %all-gather.22.cloned.1.call-update) | async-done | bytes 16777232 | tf_op jit(solution)/shard_map/all_gather | solution.py:132
  648.8 22.9 multiply_convert_fusion
  671.7 18.1 fusion.169
  715.2 15.7 convolution_convert_fusion.1
  730.9 15.4 fusion.168
  746.3 18.2 convolution_bitcast_fusion
  901.1 19.0 reduce-scatter.9.cloned.1.call-done
  925.7 67.2 %pad_maximum_fusion = f32[2048,12288]{1,0:T(8,128)} fusion(f32[2048,4096]{1,0:T(8,128)} %convolution_bitcast_fusion, f32[2048,4096]{1,0:T(8,128)} %fusion.169, f32[2048,4096]{1,0:T(8,128)} %fusion.168), kind=kLoop, calls=%fused_computation | loop fusion | flops 50331648 | bytes 201326592 | tf_op jit(solution)/shard_map/concatenate | solution.py:221
  1034.9 65.3 %all-reduce.4 = (f32[2048]{0:T(1024)S(1)}, f32[2048]{0:T(1024)S(1)}) all-reduce(f32[2048]{0:T(1024)S(1)} %get-tuple-element.13, f32[2048]{0:T(1024)S(1)} %copy-done.59), channel_id=4, replica_groups=mesh['dp'=4,'seq'=4,'tensor'=2] {'dp','seq'}, use_global_device_ids=true, to_apply=%region_23.24.clone | all-reduce | flops 4096 | bytes 32768
  1109.5 1568.5 %all-reduce.15.cloned.1.call-done = f32[2048,12288]{1,0:T(8,128)} async-done(((f32[2048,12288]{1,0:T(8,128)}), f32[2048,12288]{1,0:T(8,128)}) %all-reduce.15.cloned.1.call-update) | async-done | bytes 100663312
  2684.8 58.8 %reduce-scatter.13.cloned.1.call-done = f32[128,256]{1,0:T(8,128)} async-done(((f32[2048,256]{1,0:T(8,128)}), f32[128,256]{1,0:T(8,128)}) %reduce-scatter.13.cloned.1.call-update) | async-done | bytes 131088 | tf_op jit(solution)/shard_map/reduce_scatter | solution.py:316
  2743.6 65.0 %reduce-scatter.15.cloned.1.call-done = f32[128,256]{1,0:T(8,128)} async-done(((f32[2048,256]{1,0:T(8,128)}), f32[128,256]{1,0:T(8,128)}) %reduce-scatter.15.cloned.1.call-update) | async-done | bytes 131088 | tf_op jit(solution)/shard_map/reduce_scatter | solution.py:317
  2808.6 106.9 %reduce-scatter.11.cloned.1.call-done = f32[128,1024]{1,0:T(8,128)} async-done(((f32[2048,1024]{1,0:T(8,128)}), f32[128,1024]{1,0:T(8,128)}) %reduce-scatter.11.cloned.1.call-update) | async-done | bytes 524304 | tf_op jit(solution)/shard_map/reduce_scatter | solution.py:315
  2915.5 107.6 %reduce-scatter.17.cloned.1.call-done = f32[128,1024]{1,0:T(8,128)} async-done(((f32[2048,1024]{1,0:T(8,128)}), f32[128,1024]{1,0:T(8,128)}) %reduce-scatter.17.cloned.1.call-update) | async-done | bytes 524304 | tf_op jit(solution)/shard_map/reduce_scatter | solution.py:318
  (326 shorter events, 334.5 us)
Async XLA Ops:
  7.2 46.8 %copy-start.2 = (bf16[512,2048]{1,0:T(8,128)(2,1)S(1)}, bf16[512,2048]{1,0:T(8,128)(2,1)}, u32[]{:S(2)}) copy-start(bf16[512,2048]{1,0:T(8,128)(2,1)} %param.13) | copy-start | bytes 6291460
  7.2 46.8 %all-gather.12.cloned.1.call-start = ((), (), s32[]{:S(2)}) async-start(), calls=%async_computation.7 | async-start | bytes 1114112 | tf_op jit(solution)/shard_map/all_gather | solution.py:131
  9.0 82.7 %all-gather.10.cloned.1.call-start = ((), (), s32[]{:S(2)}) async-start(), calls=%async_computation.6 | async-start | bytes 1114112 | tf_op jit(solution)/shard_map/all_gather | solution.py:131
  10.6 135.1 %all-gather.14.cloned.1.call-start = ((), (), s32[]{:S(2)}) async-start(), calls=%async_computation.8 | async-start | bytes 4456448 | tf_op jit(solution)/shard_map/all_gather | solution.py:131
  12.4 184.9 %all-gather.16.cloned.1.call-start = ((), (), s32[]{:S(2)}) async-start(), calls=%async_computation.9 | async-start | bytes 4456448 | tf_op jit(solution)/shard_map/all_gather | solution.py:131
  14.3 250.6 %all-reduce.11.cloned.1.call-start = ((), (), s32[]{:S(2)}) async-start(), calls=%async_computation.10 | async-start | bytes 4194304 | tf_op jit(solution)/shard_map/psum | solution.py:188
  48.9 96.8 %copy-start.54 = (f32[16,1,128]{2,1,0:T(1,128)}, f32[16,1,128]{2,1,0:T(1,128)S(1)}, u32[]{:S(2)}) copy-start(f32[16,1,128]{2,1,0:T(1,128)S(1)} %convert_element_type.232) | copy-start | bytes 24580
  51.0 94.7 %copy-start.60 = (f32[512]{0:T(512)}, f32[512]{0:T(512)S(1)}, u32[]{:S(2)}) copy-start(f32[512]{0:T(512)S(1)} %add_rsqrt_fusion.1) | copy-start | bytes 6148
  51.5 99.1 %copy-start.18 = (f32[512,64]{0,1:T(8,128)}, f32[512,64]{0,1:T(8,128)S(1)}, u32[]{:S(2)}) copy-start(f32[512,64]{0,1:T(8,128)S(1)} %get-tuple-element.40) | copy-start | bytes 393220
  56.4 113.0 %copy-start.11 = (bf16[256,4,64]{0,2,1:T(8,128)(2,1)}, bf16[256,4,64]{0,2,1:T(8,128)(2,1)S(1)}, u32[]{:S(2)}) copy-start(bf16[256,4,64]{0,2,1:T(8,128)(2,1)S(1)} %get-tuple-element.38) | copy-start | bytes 393220
  72.7 96.7 %copy-start.7 = (bf16[1024,256]{0,1:T(8,128)(2,1)}, bf16[1024,256]{0,1:T(8,128)(2,1)S(1)}, u32[]{:S(2)}) copy-start(bf16[1024,256]{0,1:T(8,128)(2,1)S(1)} %all_gather.46) | copy-start | bytes 1572868
  203.2 190.7 %all-gather.18.cloned.1.call-start = ((), (), s32[]{:S(2)}) async-start(), calls=%async_computation.11 | async-start | bytes 17825792 | tf_op jit(solution)/shard_map/all_gather | solution.py:132
  206.0 315.4 %all-gather.20.cloned.1.call-start = ((), (), s32[]{:S(2)}) async-start(), calls=%async_computation.12 | async-start | bytes 17825792 | tf_op jit(solution)/shard_map/all_gather | solution.py:132
  209.7 439.1 %all-gather.22.cloned.1.call-start = ((), (), s32[]{:S(2)}) async-start(), calls=%async_computation.13 | async-start | bytes 17825792 | tf_op jit(solution)/shard_map/all_gather | solution.py:132
  212.5 564.0 %all-reduce.13.cloned.1.call-start = ((), (), s32[]{:S(2)}) async-start(), calls=%async_computation.14 | async-start | bytes 4194304 | tf_op jit(solution)/shard_map/psum | solution.py:210
  408.9 239.9 %copy-start.35 = (bf16[512,2048]{1,0:T(8,128)(2,1)S(1)}, bf16[512,2048]{1,0:T(8,128)(2,1)}, u32[]{:S(2)}) copy-start(bf16[512,2048]{1,0:T(8,128)(2,1)} %param.14) | copy-start | bytes 6291460
  715.1 182.0 %reduce-scatter.7.cloned.1.call-start = ((), (), s32[]{:S(2)}) async-start(), calls=%async_computation.15 | async-start | bytes 655360 | tf_op jit(solution)/shard_map/reduce_scatter | solution.py:274
  875.1 45.0 %reduce-scatter.9.cloned.1.call-start = ((), (), s32[]{:S(2)}) async-start(), calls=%async_computation.16 | async-start | bytes 655360 | tf_op jit(solution)/shard_map/reduce_scatter | solution.py:277
  881.3 150.7 %all-reduce.17.cloned.1.call-start = ((), (), s32[]{:S(2)}) async-start(), calls=%async_computation.22 | async-start | bytes 8388608 | tf_op jit(solution)/shard_map/psum | solution.py:198
  925.7 1752.3 %all-reduce.15.cloned.1.call-start = ((), (), s32[]{:S(2)}) async-start(), calls=%async_computation.21 | async-start | bytes 201326592
  993.0 1750.6 %reduce-scatter.13.cloned.1.call-start = ((), (), s32[]{:S(2)}) async-start(), calls=%async_computation.18 | async-start | bytes 2228224 | tf_op jit(solution)/shard_map/reduce_scatter | solution.py:316
  997.0 1811.6 %reduce-scatter.15.cloned.1.call-start = ((), (), s32[]{:S(2)}) async-start(), calls=%async_computation.19 | async-start | bytes 2228224 | tf_op jit(solution)/shard_map/reduce_scatter | solution.py:317
  999.6 1915.9 %reduce-scatter.11.cloned.1.call-start = ((), (), s32[]{:S(2)}) async-start(), calls=%async_computation.17 | async-start | bytes 8912896 | tf_op jit(solution)/shard_map/reduce_scatter | solution.py:315
  1005.6 2017.5 %reduce-scatter.17.cloned.1.call-start = ((), (), s32[]{:S(2)}) async-start(), calls=%async_computation.20 | async-start | bytes 8912896 | tf_op jit(solution)/shard_map/reduce_scatter | solution.py:318
  (76 other events, 771.9 us)
Sparse Core Ops, SparseCore 0:
  10.8 40.5 all-gather.11
  54.2 37.3 all-gather.9
  94.5 51.1 all-gather.13
  148.3 48.9 all-gather.15
  203.4 61.4 all-reduce.10
  267.5 126.4 all-gather.17
  396.8 124.5 all-gather.19
  524.2 124.5 all-gather.21
  715.3 61.1 all-reduce.12
  875.2 21.8 reduce-scatter.6
  900.0 20.0 reduce-scatter.8
  925.8 106.1 all-reduce.16
  1036.3 1641.6 all-reduce.14
  2682.2 61.3 reduce-scatter.12
  2747.8 60.7 reduce-scatter.14
  2813.1 102.3 reduce-scatter.10
  2920.0 103.0 reduce-scatter.16
where the time goes:
time: 3030 us
  waiting for transfers between devices  2380 us (79%)
  matrix products  287 us (9%)
  other arithmetic  165 us (5%)
  blocking collectives  165 us (5%)
    unnamed x18, waiting for transfers between devices  1570 us
    all_gather x3, waiting for transfers between devices, local(): lax.all_gather(for_sending(mlp_pack()), ('dp', 'seq'), axis=0, tiled=True)  349 us
    reduce_scatter x1, waiting for transfers between devices, local(): lax.psum_scatter(attn_terms[4], ('dp', 'seq'), scatter_dimension=0, tiled...  108 us
    reduce_scatter x1, waiting for transfers between devices, local(): lax.psum_scatter(attn_terms[1], ('dp', 'seq'), scatter_dimension=0, tiled...  107 us
    dot_general x7, matrix products, transposed_times(): lax.dot_general(left_side, right_side, (((0,), (0,)), ((), ())), preferre...  72.6 us
    concatenate x1, other arithmetic, local(): jnp.concatenate([transposed_times(normed_two, grad_gate), transposed_time...  67.2 us
    unnamed x1, blocking collectives  65.3 us
    reduce_scatter x1, waiting for transfers between devices, local(): lax.psum_scatter(attn_terms[3], ('dp', 'seq'), scatter_dimension=0, tiled...  65 us
  transfers between devices with their start and end apart: 17, of which 16 were waited for; matrix products, arithmetic and copies ran while one was open for 9% of the time, Pallas kernels for 0%

commit v1 on v0

--- a/solution.py
+++ b/solution.py
@@ -199,8 +199,6 @@
         times_transposed(hidden, mlp_set[3]).astype(jnp.bfloat16), "tensor"
     ).astype(jnp.float32)
     output = result.astype(jnp.bfloat16)
-    attn_set = lax.all_gather(for_sending(attn_pack()), ("dp", "seq"), axis=0, tiled=True)
-    mlp_set = lax.all_gather(for_sending(mlp_pack()), ("dp", "seq"), axis=0, tiled=True)
     grad_out = out_grad.astype(jnp.float32)
     grad_hidden = jnp.dot(out_grad, mlp_set[3], preferred_element_type=jnp.float32)
     grad_gate = (
@@ -217,20 +215,14 @@
     grad_middle = grad_out + norm_back(
         grad_normed_two, unit_two, rms_two, mlp_set[0].astype(jnp.float32)
     )
-    mlp_grads = lax.psum_scatter(
-        jnp.concatenate(
-            [
-                transposed_times(normed_two, grad_gate),
-                transposed_times(normed_two, grad_up),
-                transposed_times(out_grad, hidden),
-            ],
-            axis=1,
-        ),
-        ("dp", "seq"),
-        scatter_dimension=0,
-        tiled=True,
-    )
-    ff_local = gate_weight.shape[1]
+    def summed(term):
+        return lax.psum_scatter(
+            term.astype(jnp.bfloat16), ("dp", "seq"), scatter_dimension=0, tiled=True
+        ).astype(jnp.float32)
+
+    down_grad = summed(transposed_times(out_grad, hidden))
+    gate_grad = summed(transposed_times(normed_two, grad_gate))
+    up_grad = summed(transposed_times(normed_two, grad_up))
     grad_branch = grad_middle.astype(jnp.bfloat16)
     grad_attended = (
         jnp.dot(grad_branch, attn_set[4], preferred_element_type=jnp.float32)
@@ -312,10 +304,10 @@
     )
     attn_grads = (
         lax.psum_scatter(attn_terms[0], ("dp", "seq"), scatter_dimension=0, tiled=True),
-        lax.psum_scatter(attn_terms[1], ("dp", "seq"), scatter_dimension=0, tiled=True),
-        lax.psum_scatter(attn_terms[2], ("dp", "seq"), scatter_dimension=0, tiled=True),
-        lax.psum_scatter(attn_terms[3], ("dp", "seq"), scatter_dimension=0, tiled=True),
-        lax.psum_scatter(attn_terms[4], ("dp", "seq"), scatter_dimension=0, tiled=True),
+        summed(attn_terms[1]),
+        summed(attn_terms[2]),
+        summed(attn_terms[3]),
+        summed(attn_terms[4]),
         lax.psum_scatter(attn_terms[5], ("dp", "seq"), scatter_dimension=0, tiled=True),
     )
     return (
@@ -327,9 +319,9 @@
         attn_grads[3],
         attn_grads[4],
         attn_grads[5],
-        mlp_grads[:, :ff_local],
-        mlp_grads[:, ff_local : 2 * ff_local],
-        mlp_grads[:, 2 * ff_local :],
+        gate_grad,
+        up_grad,
+        down_grad,
     )
 
 

time: 3030 us -> 1820 us (0.60)
  waiting for transfers between devices: 2380 us -> 1200 us
  other arithmetic: 165 us -> 112 us
    unnamed x18 -> x20, waiting for transfers between devices: 1570 us -> 179 us
    reduce_scatter x4 -> x6, waiting for transfers between devices: 338 us -> 450 us  [summed(): lax.psum_scatter(term.astype(jnp.bfloat16), ('dp', 'seq'), scatter_dimens...]
    psum x1, waiting for transfers between devices: 13.2 us -> 108 us  [local(): lax.psum(times_transposed(hidden, mlp_set[3]).astype(jnp.bfloat16), 'tens...]
    concatenate x1 -> x0, other arithmetic: 67.2 us -> none  [local(): jnp.concatenate([transposed_times(normed_two, grad_gate), transposed_time...]
    psum x1, waiting for transfers between devices: 11.9 us -> 45.5 us  [local(): lax.psum((times_transposed(grad_gate, mlp_set[1]) + times_transposed(grad...]
  transfers between devices with their start and end apart: 17 -> 19, of which waited for: 16 -> 15; matrix products, arithmetic and copies ran while one was open for 9% -> 17% of each run, Pallas kernels for 0% -> 0%
where the time goes in v1:
time: 1820 us; the launch traced here: 1810 us
  waiting for transfers between devices  1200 us (66%)
  matrix products  270 us (15%)
  blocking collectives  162 us (9%)
  other arithmetic  112 us (6%)
  local copies, waits for them, and re-layouts  44.3 us (2%)
    reduce_scatter x6, waiting for transfers between devices, summed(): lax.psum_scatter(term.astype(jnp.bfloat16), ('dp', 'seq'), scatter_dimens...  450 us
    all_gather x3, waiting for transfers between devices, local(): lax.all_gather(for_sending(mlp_pack()), ('dp', 'seq'), axis=0, tiled=True)  349 us
    unnamed x20, waiting for transfers between devices  179 us
    psum x1, waiting for transfers between devices, local(): lax.psum(times_transposed(hidden, mlp_set[3]).astype(jnp.bfloat16), 'tens...  108 us
    dot_general x7, matrix products, transposed_times(): lax.dot_general(left_side, right_side, (((0,), (0,)), ((), ())), preferre...  63.4 us
    unnamed x1, blocking collectives  62.4 us
    dot_general x7, matrix products, times_transposed(): lax.dot_general(left_side, right_side, (((1,), (1,)), ((), ())), preferre...  56.9 us
    all_gather x4, waiting for transfers between devices, local(): lax.all_gather(for_sending(attn_pack()), ('dp', 'seq'), axis=0, tiled=True)  47.7 us
  transfers between devices with their start and end apart: 19, of which 15 were waited for; matrix products, arithmetic and copies ran while one was open for 17% of the time, Pallas kernels for 0%

profile of v1, /device:TPU:0, one launch (start us, length us, event | category | flops | bytes accessed | tf_op | source)
XLA Modules:
  0.0 1811.2 jit_solution(7538030029307712680)
XLA Ops:
  18.5 33.9 %all-gather = bf16[16,1,128]{2,1,0:T(2,128)(2,1)S(1)} all-gather(bf16[1,1,128]{2,1,0:T(2,128)(2,1)S(1)} %convert_bitcast_fusion.2), channel_id=1, replica_groups=mesh['dp'=4,'seq'=4,'tensor'=2] {'dp','seq'}, dimensions={0}, use_global_device_ids=true | all-gather | bytes 4352 | tf_op jit(solution)/shard_map/all_gather | solution.py:131
  57.3 15.7 all_gather.35
  76.1 15.8 all-gather.12.cloned.1.call-done
  94.3 19.1 %all_gather.37 = bf16[1024,256]{0,1:T(8,128)(2,1)S(1)} all-gather(bf16[256,256]{0,1:T(8,128)(2,1)S(1)} %bitcast.279), channel_id=1, replica_groups=mesh['dp'=4,'seq'=4,'tensor'=2] {'seq'}, dimensions={0}, use_global_device_ids=true | all-gather | bytes 655360 | tf_op jit(solution)/shard_map/all_gather | solution.py:152
  114.1 31.9 %all-gather.14.cloned.1.call-done = bf16[2048,1024]{1,0:T(8,128)(2,1)} async-done(((bf16[128,1024]{1,0:T(8,128)(2,1)}), bf16[2048,1024]{1,0:T(8,128)(2,1)}) %all-gather.14.cloned.1.call-update) | async-done | bytes 4194320 | tf_op jit(solution)/shard_map/all_gather | solution.py:131
  212.9 31.2 %all-gather.1 = bf16[16,1,128]{2,1,0:T(2,128)(2,1)S(1)} all-gather(bf16[1,1,128]{2,1,0:T(2,128)(2,1)S(1)} %convert_bitcast_fusion.1), channel_id=1, replica_groups=mesh['dp'=4,'seq'=4,'tensor'=2] {'dp','seq'}, dimensions={0}, use_global_device_ids=true | all-gather | bytes 4352 | tf_op jit(solution)/shard_map/all_gather | solution.py:132
  246.6 20.1 %all-reduce.9.cloned.1.call-done = bf16[512,2048]{1,0:T(8,128)(2,1)} async-done(((bf16[512,2048]{1,0:T(8,128)(2,1)}), bf16[512,2048]{1,0:T(8,128)(2,1)}) %all-reduce.9.cloned.1.call-update) | async-done | bytes 2097168 | tf_op jit(solution)/shard_map/psum | solution.py:188
  271.6 124.2 %all-gather.20.cloned.1.call-done = bf16[2048,4096]{1,0:T(8,128)(2,1)} async-done(((bf16[128,4096]{1,0:T(8,128)(2,1)}), bf16[2048,4096]{1,0:T(8,128)(2,1)}) %all-gather.20.cloned.1.call-update) | async-done | bytes 16777232 | tf_op jit(solution)/shard_map/all_gather | solution.py:132
  395.8 15.2 fusion.159
  411.0 112.2 %all-gather.18.cloned.1.call-done = bf16[2048,4096]{1,0:T(8,128)(2,1)} async-done(((bf16[128,4096]{1,0:T(8,128)(2,1)}), bf16[2048,4096]{1,0:T(8,128)(2,1)}) %all-gather.18.cloned.1.call-update) | async-done | bytes 16777232 | tf_op jit(solution)/shard_map/all_gather | solution.py:132
  523.2 15.1 fusion.158
  538.3 112.4 %all-gather.22.cloned.1.call-done = bf16[2048,4096]{1,0:T(8,128)(2,1)} async-done(((bf16[128,4096]{1,0:T(8,128)(2,1)}), bf16[2048,4096]{1,0:T(8,128)(2,1)}) %all-gather.22.cloned.1.call-update) | async-done | bytes 16777232 | tf_op jit(solution)/shard_map/all_gather | solution.py:132
  650.6 22.2 %multiply_convert_fusion = (bf16[512,4096]{1,0:T(8,128)(2,1)}, bf16[512,4096]{1,0:T(8,128)(2,1)}, bf16[512,4096]{1,0:T(8,128)(2,1)}) fusion(f32[512,4096]{1,0:T(8,128)} %fusion.158, f32[512,4096]{1,0:T(8,128)} %fusion.159, bf16[512,2048]{1,0:T(8,128)(2,1)} %param.14, bf16[2048,4096]{1,0:T(8,128)(2,1)} %all-gather.22.cloned.1.call-done), kind=kOutput, calls=%fused_computation.43 | convolution fusion | flops 8621391872 | bytes 48234496 | tf_op jit(solution)/shard_map/dot_general | solution.py:203
  672.8 15.4 fusion.160
  702.5 15.7 convolution_convert_fusion.5
  718.3 45.5 %all-reduce.11.cloned.1.call-done = bf16[512,2048]{1,0:T(8,128)(2,1)} async-done(((bf16[512,2048]{1,0:T(8,128)(2,1)}), bf16[512,2048]{1,0:T(8,128)(2,1)}) %all-reduce.11.cloned.1.call-update) | async-done | bytes 2097168 | tf_op jit(solution)/shard_map/psum | solution.py:208
  923.8 21.0 %copy.109 = bf16[2048,4096]{1,0:T(8,128)(2,1)} copy(bf16[2048,4096]{0,1:T(8,128)(2,1)} %convert_bitcast_fusion) | data formatting | bytes 33554432
  978.6 19.4 %reduce-scatter.18.cloned.1.call-done = bf16[128,256]{1,0:T(8,128)(2,1)} async-done(((bf16[2048,256]{1,0:T(8,128)(2,1)}), bf16[128,256]{1,0:T(8,128)(2,1)}) %reduce-scatter.18.cloned.1.call-update) | async-done | bytes 65552 | tf_op jit(solution)/shard_map/reduce_scatter | solution.py:219
  999.5 108.4 %all-reduce.13.cloned.1.call-done = (bf16[512,2048]{1,0:T(8,128)(2,1)}, bf16[512,2048]{1,0:T(8,128)(2,1)}) async-done(((bf16[512,2048]{1,0:T(8,128)(2,1)}, bf16[512,2048]{1,0:T(8,128)(2,1)}), (bf16[512,2048]{1,0:T(8,128)(2,1)}, bf16[512,2048]{1,0:T(8,128)(2,1)})) %all-reduce.13.cloned.1.call-update) | async-done | bytes 4194320 | tf_op jit(solution)/shard_map/psum | solution.py:198
  1110.8 62.4 %all-reduce.3 = (f32[2048]{0:T(1024)S(1)}, f32[2048]{0:T(1024)S(1)}) all-reduce(f32[2048]{0:T(1024)S(1)} %get-tuple-element.46, f32[2048]{0:T(1024)S(1)} %copy-done.54), channel_id=4, replica_groups=mesh['dp'=4,'seq'=4,'tensor'=2] {'dp','seq'}, use_global_device_ids=true, to_apply=%region_23.24.clone | all-reduce | flops 4096 | bytes 32768
  1186.4 73.8 %reduce-scatter.16.cloned.1.call-done = bf16[128,1024]{1,0:T(8,128)(2,1)} async-done(((bf16[2048,1024]{1,0:T(8,128)(2,1)}), bf16[128,1024]{1,0:T(8,128)(2,1)}) %reduce-scatter.16.cloned.1.call-update) | async-done | bytes 262160 | tf_op jit(solution)/shard_map/reduce_scatter | solution.py:219
  1262.0 178.6 %reduce-scatter.28.cloned.1.call-done = bf16[128,4096]{1,0:T(8,128)(2,1)} async-done(((bf16[2048,4096]{1,0:T(8,128)(2,1)}), bf16[128,4096]{1,0:T(8,128)(2,1)}) %reduce-scatter.28.cloned.1.call-update) | async-done | bytes 1048592
  1443.9 177.2 %reduce-scatter.26.cloned.1.call-done = bf16[128,4096]{1,0:T(8,128)(2,1)} async-done(((bf16[2048,4096]{1,0:T(8,128)(2,1)}), bf16[128,4096]{1,0:T(8,128)(2,1)}) %reduce-scatter.26.cloned.1.call-update) | async-done | bytes 1048592 | tf_op jit(solution)/shard_map/reduce_scatter | solution.py:219
  1623.8 177.8 %reduce-scatter.24.cloned.1.call-done = bf16[128,4096]{1,0:T(8,128)(2,1)} async-done(((bf16[2048,4096]{1,0:T(8,128)(2,1)}), bf16[128,4096]{1,0:T(8,128)(2,1)}) %reduce-scatter.24.cloned.1.call-update) | async-done | bytes 1048592 | tf_op jit(solution)/shard_map/reduce_scatter | solution.py:219
  (341 shorter events, 330.8 us)
Async XLA Ops:
  7.2 48.1 %all-gather.10.cloned.1.call-start = ((), (), s32[]{:S(2)}) async-start(), calls=%async_computation.9 | async-start | bytes 1114112 | tf_op jit(solution)/shard_map/all_gather | solution.py:131
  9.0 82.9 %all-gather.12.cloned.1.call-start = ((), (), s32[]{:S(2)}) async-start(), calls=%async_computation.10 | async-start | bytes 1114112 | tf_op jit(solution)/shard_map/all_gather | solution.py:131
  10.6 135.3 %all-gather.14.cloned.1.call-start = ((), (), s32[]{:S(2)}) async-start(), calls=%async_computation.11 | async-start | bytes 4456448 | tf_op jit(solution)/shard_map/all_gather | solution.py:131
  12.4 185.8 %all-gather.16.cloned.1.call-start = ((), (), s32[]{:S(2)}) async-start(), calls=%async_computation.12 | async-start | bytes 4456448 | tf_op jit(solution)/shard_map/all_gather | solution.py:131
  14.3 252.4 %all-reduce.9.cloned.1.call-start = ((), (), s32[]{:S(2)}) async-start(), calls=%async_computation.13 | async-start | bytes 4194304 | tf_op jit(solution)/shard_map/psum | solution.py:188
  18.5 127.4 %copy-start.55 = (f32[512]{0:T(512)}, f32[512]{0:T(512)S(1)}, u32[]{:S(2)}) copy-start(f32[512]{0:T(512)S(1)} %add_rsqrt_fusion.1) | copy-start | bytes 6148
  52.4 93.5 %copy-start.52 = (f32[16,1,128]{2,1,0:T(1,128)}, f32[16,1,128]{2,1,0:T(1,128)S(1)}, u32[]{:S(2)}) copy-start(f32[16,1,128]{2,1,0:T(1,128)S(1)} %convert_element_type.283) | copy-start | bytes 24580
  54.0 96.8 %copy-start.16 = (f32[512,64]{0,1:T(8,128)}, f32[512,64]{0,1:T(8,128)S(1)}, u32[]{:S(2)}) copy-start(f32[512,64]{0,1:T(8,128)S(1)} %get-tuple-element.70) | copy-start | bytes 393220
  94.3 73.3 %copy-start.10 = (bf16[256,4,64]{0,2,1:T(8,128)(2,1)}, bf16[256,4,64]{0,2,1:T(8,128)(2,1)S(1)}, u32[]{:S(2)}) copy-start(bf16[256,4,64]{0,2,1:T(8,128)(2,1)S(1)} %get-tuple-element.68) | copy-start | bytes 393220
  204.5 191.3 %all-gather.20.cloned.1.call-start = ((), (), s32[]{:S(2)}) async-start(), calls=%async_computation.15 | async-start | bytes 17825792 | tf_op jit(solution)/shard_map/all_gather | solution.py:132
  207.3 315.9 %all-gather.18.cloned.1.call-start = ((), (), s32[]{:S(2)}) async-start(), calls=%async_computation.14 | async-start | bytes 17825792 | tf_op jit(solution)/shard_map/all_gather | solution.py:132
  210.1 440.6 %all-gather.22.cloned.1.call-start = ((), (), s32[]{:S(2)}) async-start(), calls=%async_computation.16 | async-start | bytes 17825792 | tf_op jit(solution)/shard_map/all_gather | solution.py:132
  212.8 550.9 %all-reduce.11.cloned.1.call-start = ((), (), s32[]{:S(2)}) async-start(), calls=%async_computation.17 | async-start | bytes 4194304 | tf_op jit(solution)/shard_map/psum | solution.py:208
  702.5 162.0 %reduce-scatter.14.cloned.1.call-start = ((), (), s32[]{:S(2)}) async-start(), calls=%async_computation.19 | async-start | bytes 655360 | tf_op jit(solution)/shard_map/reduce_scatter | solution.py:269
  811.7 65.9 %reduce-scatter.12.cloned.1.call-start = ((), (), s32[]{:S(2)}) async-start(), calls=%async_computation.18 | async-start | bytes 655360 | tf_op jit(solution)/shard_map/reduce_scatter | solution.py:266
  855.7 121.4 %reduce-scatter.20.cloned.1.call-start = ((), (), s32[]{:S(2)}) async-start(), calls=%async_computation.22 | async-start | bytes 1114112 | tf_op jit(solution)/shard_map/reduce_scatter | solution.py:219
  867.5 130.4 %reduce-scatter.18.cloned.1.call-start = ((), (), s32[]{:S(2)}) async-start(), calls=%async_computation.21 | async-start | bytes 1114112 | tf_op jit(solution)/shard_map/reduce_scatter | solution.py:219
  883.4 224.5 %all-reduce.13.cloned.1.call-start = ((), (), s32[]{:S(2)}) async-start(), calls=%async_computation.27 | async-start | bytes 8388608 | tf_op jit(solution)/shard_map/psum | solution.py:198
  892.9 291.8 %reduce-scatter.22.cloned.1.call-start = ((), (), s32[]{:S(2)}) async-start(), calls=%async_computation.23 | async-start | bytes 4456448 | tf_op jit(solution)/shard_map/reduce_scatter | solution.py:219
  902.9 357.3 %reduce-scatter.16.cloned.1.call-start = ((), (), s32[]{:S(2)}) async-start(), calls=%async_computation.20 | async-start | bytes 4456448 | tf_op jit(solution)/shard_map/reduce_scatter | solution.py:219
  908.8 531.9 %reduce-scatter.28.cloned.1.call-start = ((), (), s32[]{:S(2)}) async-start(), calls=%async_computation.26 | async-start | bytes 17825792
  944.8 676.3 %reduce-scatter.26.cloned.1.call-start = ((), (), s32[]{:S(2)}) async-start(), calls=%async_computation.25 | async-start | bytes 17825792 | tf_op jit(solution)/shard_map/reduce_scatter | solution.py:219
  959.9 841.8 %reduce-scatter.24.cloned.1.call-start = ((), (), s32[]{:S(2)}) async-start(), calls=%async_computation.24 | async-start | bytes 17825792 | tf_op jit(solution)/shard_map/reduce_scatter | solution.py:219
  975.2 135.6 %copy-start.54 = (f32[2048]{0:T(1024)S(1)}, f32[2048]{0:T(1024)}, u32[]{:S(2)}) copy-start(f32[2048]{0:T(1024)} %get-tuple-element.44) | copy-start | bytes 24580
  (78 other events, 781.5 us)
Sparse Core Ops, SparseCore 0:
  10.8 40.5 all-gather.9
  54.2 37.6 all-gather.11
  94.7 51.2 all-gather.13
  148.6 48.8 all-gather.15
  204.6 62.0 all-reduce.8
  269.3 126.4 all-gather.19
  398.6 124.5 all-gather.17
  526.0 124.5 all-gather.21
  702.6 61.1 all-reduce.10
  811.9 21.8 reduce-scatter.13
  855.8 21.7 reduce-scatter.11
  881.1 55.9 reduce-scatter.19
  941.2 56.6 reduce-scatter.17
  1000.9 106.9 all-reduce.12
  1111.6 72.9 reduce-scatter.21
  1188.3 71.8 reduce-scatter.15
  1264.2 176.4 reduce-scatter.27
  1444.6 176.4 reduce-scatter.25
  1625.2 176.4 reduce-scatter.23

commit v2 on v1

v2 whole, which is shorter than its diff:
```python
import math

import jax
import jax.numpy as jnp
import numpy as np
from jax import lax
from jax.sharding import PartitionSpec as P

HEAD_DIM = 64
PROMPT = 1024
CONT_LEN = 128


epsilon = 1e-05


def rope_freqs(head_width):
    scaled_list = []
    for column in range(head_width // 2):
        inverse = 1.0 / 500000.0 ** (2.0 * column / head_width)
        wavelength = 2.0 * math.pi / inverse
        if wavelength < 2048.0:
            scaled_list.append(inverse)
        elif wavelength > 8192.0:
            scaled_list.append(inverse / 32.0)
        else:
            smooth_mix = (8192.0 / wavelength - 1.0) / 3.0
            scaled_list.append((1.0 - smooth_mix) * inverse / 32.0 + smooth_mix * inverse)
    return np.array(scaled_list, dtype=np.float32)


def rope_apply(values, cos_table, sin_table):
    half_width = values.shape[-1] // 2
    turned = jnp.concatenate([-values[..., half_width:], values[..., :half_width]], axis=-1)
    return values * cos_table + turned * sin_table


def rope_back(grads, cos_table, sin_table):
    half_width = grads.shape[-1] // 2
    twisted = grads * sin_table
    return grads * cos_table + jnp.concatenate(
        [twisted[..., half_width:], -twisted[..., :half_width]], axis=-1
    )


def norm_parts(values):
    inv_rms = lax.rsqrt(jnp.mean(values * values, axis=-1, keepdims=True) + epsilon)
    return (values * inv_rms, inv_rms)


def norm_back(grad_normed, unit_rows, inv_rms, gain_vec):
    grad_unit = grad_normed * gain_vec
    return inv_rms * (
        grad_unit - unit_rows * jnp.mean(grad_unit * unit_rows, axis=-1, keepdims=True)
    )


def times_transposed(left_side, right_side):
    return lax.dot_general(
        left_side, right_side, (((1,), (1,)), ((), ())), preferred_element_type=jnp.float32
    )


def transposed_times(left_side, right_side):
    return lax.dot_general(
        left_side, right_side, (((0,), (0,)), ((), ())), preferred_element_type=jnp.float32
    )


QUAD = 4


def f32(array):
    return array.astype(jnp.float32)


def bf16(array):
    return array.astype(jnp.bfloat16)


def flip(array, mask):
    return lax.ppermute(array, "dp", [(i, i ^ mask) for i in range(lax.axis_size("dp"))])


def shift(array, step):
    count = lax.axis_size("seq")
    return lax.ppermute(array, "seq", [(i, (i + step) % count) for i in range(count)])


def pair_sum(array):
    count = lax.axis_size("tensor")
    if count != 2:
        return lax.psum(f32(array), "tensor")
    return f32(array) + f32(lax.ppermute(array, "tensor", [(0, 1), (1, 0)]))


def far_groups():
    count = lax.axis_size("dp")
    return [list(range(low, count, QUAD)) for low in range(QUAD)]


def far_gather(array):
    if lax.axis_size("dp") == QUAD:
        return array
    return lax.all_gather(array, "dp", axis=0, tiled=True, axis_index_groups=far_groups())


def far_scatter(array):
    if lax.axis_size("dp") == QUAD:
        return array
    return lax.psum_scatter(
        array, "dp", scatter_dimension=0, tiled=True, axis_index_groups=far_groups()
    )


def mirror(pieces, rank):
    odd, upper = (rank & 1) == 1, (rank & 2) == 2
    a, b, c, d = pieces
    a, b, c, d = (
        jnp.where(odd, b, a),
        jnp.where(odd, a, b),
        jnp.where(odd, d, c),
        jnp.where(odd, c, d),
    )
    return [
        jnp.where(upper, c, a),
        jnp.where(upper, d, b),
        jnp.where(upper, a, c),
        jnp.where(upper, b, d),
    ]


def mirror_columns(array, rank):
    blocks = lax.axis_size("dp")
    width = array.shape[1] // blocks
    cut = [array[:, i * width : (i + 1) * width] for i in range(blocks)]
    moved = []
    for first in range(0, blocks, QUAD):
        moved += mirror(cut[first : first + QUAD], rank)
    return jnp.concatenate(moved, axis=1)


def columns_swapped(array, outer, inner):
    far = lax.axis_size("dp") // QUAD
    width = array.shape[1] // (far * outer * inner)
    cut = []
    for f in range(far):
        for i in range(inner):
            for o in range(outer):
                start = ((f * outer + o) * inner + i) * width
                cut.append(array[:, start : start + width])
    return jnp.concatenate(cut, axis=1)


def quad_pieces(array):
    upper = flip(array, 2)
    return [array, flip(array, 1), upper, flip(upper, 1)]


def quad_sum(pieces):
    near = [
        bf16(f32(pieces[0]) + f32(flip(bf16(pieces[1]), 1))),
        bf16(f32(pieces[2]) + f32(flip(bf16(pieces[3]), 1))),
    ]
    return bf16(f32(near[0]) + f32(flip(near[1], 2)))


def attn_gathered(block):
    far = lax.axis_size("dp") // QUAD
    pieces = quad_pieces(far_gather(lax.all_gather(block, "seq", axis=0, tiled=True)))
    if far == 1:
        return jnp.concatenate(pieces, axis=0)
    cut = [p.reshape(far, -1, p.shape[1]) for p in pieces]
    return jnp.stack(cut, axis=1).reshape(-1, block.shape[1])


def attn_scattered(term):
    far = lax.axis_size("dp") // QUAD
    width = term.shape[1]
    cut = term.reshape(far, QUAD, -1, width)
    near = quad_sum([cut[:, k].reshape(-1, width) for k in range(QUAD)])
    return f32(
        lax.psum_scatter(far_scatter(near), "seq", scatter_dimension=0, tiled=True)
    )


def mlp_gathered(weight, rank):
    rows, columns = weight.shape
    cut = weight.reshape(rows, QUAD, columns // QUAD)
    pieces = []
    for k in range(QUAD):
        part = bf16(lax.dynamic_index_in_dim(cut, rank ^ k, axis=1, keepdims=False))
        pieces.append(flip(part, k) if k else part)
    block = jnp.concatenate(mirror(pieces, rank), axis=0)
    return far_gather(lax.all_gather(block, "seq", axis=0, tiled=True))


def mlp_scattered(term, rank):
    width = term.shape[1]
    own = lax.psum_scatter(
        far_scatter(bf16(term)), "seq", scatter_dimension=0, tiled=True
    ).reshape(QUAD, -1, width)
    pieces = []
    for k in range(QUAD):
        part = lax.dynamic_index_in_dim(own, rank ^ k, axis=0, keepdims=False)
        pieces.append(flip(part, k) if k else part)
    return f32(jnp.concatenate(mirror(pieces, rank), axis=1))


def local(
    tokens,
    out_grad,
    positions,
    attn_gain,
    q_weight,
    k_weight,
    v_weight,
    o_weight,
    mlp_gain,
    gate_weight,
    up_weight,
    down_weight,
):
    seq_count = lax.axis_size("seq")
    seq_rank = lax.axis_index("seq")
    rank = lax.axis_index("dp") % QUAD
    tok_rows, width = tokens.shape
    prompt_rows = PROMPT // seq_count
    cont_here = (tok_rows - prompt_rows) // CONT_LEN

    own_gains = jnp.stack([bf16(attn_gain), bf16(mlp_gain)], axis=1)
    own_gains = jnp.pad(own_gains, ((0, 0), (0, 126)))
    attn_own = jnp.concatenate(
        [bf16(q_weight), bf16(k_weight), bf16(v_weight), own_gains], axis=1
    )
    attn_all = attn_gathered(attn_own)
    o_all = attn_gathered(bf16(o_weight))
    gate_all = mlp_gathered(gate_weight, rank)
    up_all = mlp_gathered(up_weight, rank)
    down_all = mlp_gathered(down_weight, rank)
    q_cols, k_cols = q_weight.shape[1], k_weight.shape[1]
    qkv_cols = q_cols + 2 * k_cols
    qkv_all = attn_all[:, :qkv_cols]
    gains = f32(attn_all[:, qkv_cols:].T)
    gain_one, gain_two = gains[0], gains[1]

    all_pos = positions[0]
    own_pos = lax.dynamic_slice_in_dim(all_pos, seq_rank * tok_rows, tok_rows)
    row_offset = jnp.arange(tok_rows, dtype=jnp.int32)
    cont_number = 1 + seq_rank * cont_here + (row_offset - prompt_rows) // CONT_LEN
    own_seg = jnp.where(row_offset < prompt_rows, jnp.zeros_like(row_offset), cont_number)
    prompt_pos = all_pos.reshape(seq_count, tok_rows)[:, :prompt_rows].reshape(-1)
    prompt_pos = lax.dynamic_slice_in_dim(
        jnp.concatenate([prompt_pos, prompt_pos]), seq_rank * prompt_rows, PROMPT
    )
    key_pos = jnp.concatenate([prompt_pos, own_pos[prompt_rows:]])
    key_seg = jnp.concatenate([jnp.zeros_like(prompt_pos), own_seg[prompt_rows:]])
    visible = (key_pos[None, :] <= own_pos[:, None]) & (
        (key_seg[None, :] == 0) | (key_seg[None, :] == own_seg[:, None])
    )
    angles = (
        own_pos.astype(jnp.float32)[:, None]
        * jnp.asarray(rope_freqs(HEAD_DIM), jnp.float32)[None, :]
    )
    angles = jnp.concatenate([angles, angles], axis=1)
    cos_table = jnp.cos(angles)[:, None, :]
    sin_table = jnp.sin(angles)[:, None, :]
    score_scale = 1.0 / math.sqrt(HEAD_DIM)

    inputs = f32(mirror_columns(tokens, rank))
    grad_out = f32(mirror_columns(out_grad, rank))
    grad_all = jnp.concatenate(
        quad_pieces(columns_swapped(out_grad, QUAD, seq_count)), axis=0
    )
    unit_one, rms_one = norm_parts(inputs)
    normed = bf16(unit_one * gain_one)
    qkv_raw = jnp.dot(normed, qkv_all, preferred_element_type=jnp.float32)
    query_raw = qkv_raw[:, :q_cols]
    key_raw = qkv_raw[:, q_cols : q_cols + k_cols]
    values_own = bf16(qkv_raw[:, q_cols + k_cols :])
    local_heads = q_cols // HEAD_DIM
    local_kv = k_cols // HEAD_DIM
    group_size = local_heads // local_kv
    keys_own = bf16(
        rope_apply(key_raw.reshape(tok_rows, local_kv, HEAD_DIM), cos_table, sin_table)
    ).reshape(tok_rows, -1)
    own_pair = jnp.concatenate([keys_own, values_own], axis=1)
    prompt_pair = [own_pair[:prompt_rows]]
    for step in range(1, seq_count):
        prompt_pair.append(shift(own_pair[:prompt_rows], -step))
    pair_all = jnp.concatenate(prompt_pair + [own_pair[prompt_rows:]], axis=0)
    key_all = pair_all[:, :k_cols].reshape(-1, local_kv, HEAD_DIM)
    value_all = pair_all[:, k_cols:].reshape(-1, local_kv, HEAD_DIM)
    queries = bf16(
        rope_apply(query_raw.reshape(tok_rows, local_heads, HEAD_DIM), cos_table, sin_table)
    )

    def head_scores(query_group, key_group):
        scores = (
            jnp.einsum("tgd,cd->gtc", query_group, key_group, preferred_element_type=jnp.float32)
            * score_scale
        )
        return jnp.where(visible[None], scores, -1e30)

    mixed_list = []
    log_totals = []
    for kv_head in range(local_kv):
        query_group = queries[:, kv_head * group_size : (kv_head + 1) * group_size, :]
        scores = head_scores(query_group, key_all[:, kv_head, :])
        row_max = jnp.max(scores, axis=-1, keepdims=True)
        exponent = jnp.exp(scores - row_max)
        row_total = jnp.sum(exponent, axis=-1, keepdims=True)
        probability = exponent / row_total
        log_totals.append(row_max + jnp.log(row_total))
        mixed_list.append(
            jnp.einsum(
                "gtc,cd->tgd",
                bf16(probability),
                value_all[:, kv_head, :],
                preferred_element_type=jnp.float32,
            )
        )
    attended = bf16(jnp.concatenate(mixed_list, axis=1).reshape(tok_rows, -1))
    middle = inputs + pair_sum(bf16(times_transposed(attended, o_all)))
    unit_two, rms_two = norm_parts(middle)
    normed_two = bf16(unit_two * gain_two)
    normed_all = jnp.concatenate(
        quad_pieces(columns_swapped(mirror_columns(normed_two, rank), QUAD, seq_count)), axis=0
    )
    gate_pre = jnp.dot(normed_all, gate_all, preferred_element_type=jnp.float32)
    upward = jnp.dot(normed_all, up_all, preferred_element_type=jnp.float32)
    sigmoid_gate = jax.nn.sigmoid(gate_pre)
    activated = gate_pre * sigmoid_gate
    hidden = bf16(activated * upward)

    def token_sum(part):
        cut = [part[k * tok_rows : (k + 1) * tok_rows] for k in range(QUAD)]
        total = bf16(pair_sum(quad_sum(cut)))
        return mirror_columns(columns_swapped(total, seq_count, QUAD), rank)

    grad_hidden = jnp.dot(grad_all, down_all, preferred_element_type=jnp.float32)
    grad_gate = bf16(grad_hidden * upward * sigmoid_gate * (1.0 + gate_pre * (1.0 - sigmoid_gate)))
    grad_up = bf16(grad_hidden * activated)
    grad_normed_two = f32(
        token_sum(bf16(times_transposed(grad_gate, gate_all) + times_transposed(grad_up, up_all)))
    )
    down_grad = mlp_scattered(transposed_times(grad_all, hidden), rank)
    gate_grad = mlp_scattered(transposed_times(normed_all, grad_gate), rank)
    up_grad = mlp_scattered(transposed_times(normed_all, grad_up), rank)
    output = mirror_columns(
        bf16(middle + f32(token_sum(bf16(times_transposed(hidden, down_all))))), rank
    )
    grad_middle = grad_out + norm_back(grad_normed_two, unit_two, rms_two, gain_two)
    grad_branch = bf16(grad_middle)
    o_grad = attn_scattered(transposed_times(grad_branch, attended))
    grad_attended = bf16(
        jnp.dot(grad_branch, o_all, preferred_element_type=jnp.float32)
    ).reshape(tok_rows, local_heads, HEAD_DIM)
    query_grads = []
    key_grads = []
    value_grads = []
    for kv_head in range(local_kv):
        query_group = queries[:, kv_head * group_size : (kv_head + 1) * group_size, :]
        key_group = key_all[:, kv_head, :]
        value_group = value_all[:, kv_head, :]
        grad_group = grad_attended[:, kv_head * group_size : (kv_head + 1) * group_size, :]
        probability = jnp.exp(head_scores(query_group, key_group) - log_totals[kv_head])
        grad_prob = jnp.einsum(
            "tgd,cd->gtc", grad_group, value_group, preferred_element_type=jnp.float32
        )
        row_dot = jnp.sum(probability * grad_prob, axis=-1, keepdims=True)
        grad_scores = bf16(probability * (grad_prob - row_dot))
        query_grads.append(
            jnp.einsum("gtc,cd->tgd", grad_scores, key_group, preferred_element_type=jnp.float32)
            * score_scale
        )
        key_grads.append(
            jnp.einsum("gtc,tgd->cd", grad_scores, query_group, preferred_element_type=jnp.float32)
            * score_scale
        )
        value_grads.append(
            jnp.einsum(
                "gtc,tgd->cd",
                bf16(probability),
                grad_group,
                preferred_element_type=jnp.float32,
            )
        )
    grad_queries = jnp.concatenate(query_grads, axis=1)
    grad_keys = jnp.stack(key_grads, axis=1).reshape(-1, local_kv * HEAD_DIM)
    grad_values = jnp.stack(value_grads, axis=1).reshape(-1, local_kv * HEAD_DIM)
    grad_pair = jnp.concatenate([grad_keys, grad_values], axis=1)
    pair_share = grad_pair[:prompt_rows]
    for step in range(1, seq_count):
        part = grad_pair[step * prompt_rows : (step + 1) * prompt_rows]
        pair_share = pair_share + f32(shift(bf16(part), step))
    pair_own = jnp.concatenate([pair_share, grad_pair[PROMPT:]], axis=0)
    grad_query_raw = bf16(rope_back(grad_queries, cos_table, sin_table).reshape(tok_rows, -1))
    grad_key_raw = bf16(
        rope_back(
            pair_own[:, :k_cols].reshape(tok_rows, local_kv, HEAD_DIM), cos_table, sin_table
        ).reshape(tok_rows, -1)
    )
    grad_value_raw = bf16(pair_own[:, k_cols:])
    grad_raw = jnp.concatenate([grad_query_raw, grad_key_raw, grad_value_raw], axis=1)
    qkv_grad = attn_scattered(transposed_times(normed, grad_raw))
    grad_normed = pair_sum(bf16(times_transposed(grad_raw, qkv_all)))
    grad_inputs = grad_middle + norm_back(grad_normed, unit_one, rms_one, gain_one)
    tokens_grad = mirror_columns(bf16(grad_inputs), rank)

    q_grad = qkv_grad[:, :q_cols]
    k_grad = qkv_grad[:, q_cols : q_cols + k_cols]
    v_grad = qkv_grad[:, q_cols + k_cols :]

    def weighed(weight, grad):
        return jnp.sum(f32(bf16(weight)) * grad, axis=1)

    gain_sums = jnp.stack(
        [
            weighed(q_weight, q_grad) + weighed(k_weight, k_grad) + weighed(v_weight, v_grad),
            weighed(gate_weight, gate_grad) + weighed(up_weight, up_grad),
        ]
    )
    gain_sums = pair_sum(gain_sums)
    attn_gain_grad = gain_sums[0] / f32(bf16(attn_gain))
    mlp_gain_grad = gain_sums[1] / f32(bf16(mlp_gain))
    return (
        output,
        tokens_grad,
        attn_gain_grad,
        q_grad,
        k_grad,
        v_grad,
        o_grad,
        mlp_gain_grad,
        gate_grad,
        up_grad,
        down_grad,
    )


def solution(mesh):
    placed = (
        P(("dp", "seq"), None),
        P(("dp", "seq"), None),
        P("dp", None),
        P(("dp", "seq")),
        P(("dp", "seq"), "tensor"),
        P(("dp", "seq"), "tensor"),
        P(("dp", "seq"), "tensor"),
        P(("dp", "seq"), "tensor"),
        P(("dp", "seq")),
        P(("dp", "seq"), "tensor"),
        P(("dp", "seq"), "tensor"),
        P(("dp", "seq"), "tensor"),
    )
    return jax.shard_map(
        local,
        mesh=mesh,
        in_specs=placed,
        out_specs=(
            P(("dp", "seq"), None),
            P(("dp", "seq"), None),
            P(("dp", "seq")),
            P(("dp", "seq"), "tensor"),
            P(("dp", "seq"), "tensor"),
            P(("dp", "seq"), "tensor"),
            P(("dp", "seq"), "tensor"),
            P(("dp", "seq")),
            P(("dp", "seq"), "tensor"),
            P(("dp", "seq"), "tensor"),
            P(("dp", "seq"), "tensor"),
        ),
        check_vma=False,
    )
```

time: 1820 us -> 1020 us (0.56)
  waiting for transfers between devices: 1200 us -> 401 us
  blocking collectives: 162 us -> 0 us
  local copies, waits for them, and re-layouts: 44.3 us -> 126 us
  other arithmetic: 112 us -> 156 us
  starting transfers between devices: 1.58 us -> 40.9 us
    reduce_scatter x8 -> x5, waiting for transfers between devices: 455 us -> 0.03 us  [the longest x3 0.02 us: mlp_scattered(): lax.psum_scatter(far_scatter(bf16(term)), 'seq', scatter_dimension=0, til...]
    ppermute x0 -> x53, waiting for transfers between devices: none -> 345 us  [the longest x42 211 us: flip(): lax.ppermute(array, 'dp', [(i, i ^ mask) for i in range(lax.axis_size('dp...]
    all_gather x7 -> x5, waiting for transfers between devices: 397 us -> 55.4 us  [the longest x2 51.1 us: attn_gathered(): lax.all_gather(block, 'seq', axis=0, tiled=True)]
    unnamed x20 -> x10, waiting for transfers between devices: 179 us -> 0.16 us
    psum x3 -> x0, waiting for transfers between devices: 174 us -> none  [the longest x1 108 us: local(): lax.psum(times_transposed(hidden, mlp_set[3]).astype(jnp.bfloat16), 'tens...]
    all_gather x4 -> x0, blocking collectives: 99.9 us -> none  [the longest x1 33.9 us: local(): lax.all_gather(for_sending(attn_pack()), ('dp', 'seq'), axis=0, tiled=True)]
    unnamed x1 -> x0, blocking collectives: 62.4 us -> none
    ppermute x0 -> x53, starting transfers between devices: none -> 40.3 us  [the longest x42 26.2 us: flip(): lax.ppermute(array, 'dp', [(i, i ^ mask) for i in range(lax.axis_size('dp...]
  transfers between devices with their start and end apart: 19 -> 63, of which waited for: 15 -> 19; matrix products, arithmetic and copies ran while one was open for 17% -> 49% of each run, Pallas kernels for 0% -> 0%
where the time goes in v2:
time: 1020 us; the launch traced here: 1010 us
  waiting for transfers between devices  401 us (39%)
  matrix products  266 us (26%)
  other arithmetic  156 us (15%)
  local copies, waits for them, and re-layouts  126 us (12%)
  starting transfers between devices  40.9 us (4%)
  between operations  16.8 us (2%)
    ppermute x42, waiting for transfers between devices, flip(): lax.ppermute(array, 'dp', [(i, i ^ mask) for i in range(lax.axis_size('dp...  211 us
    ppermute x5, waiting for transfers between devices, pair_sum(): return f32(array) + f32(lax.ppermute(array, 'tensor', [(0, 1), (1, 0)]))  77.9 us
    convert_element_type x25, other arithmetic, bf16(): return array.astype(jnp.bfloat16)  76.3 us
    unnamed x299, local copies, waits for them, and re-layouts  66 us
    ppermute x6, waiting for transfers between devices, shift(): lax.ppermute(array, 'seq', [(i, (i + step) % count) for i in range(count)])  56.8 us
    dot_general x5, matrix products, transposed_times(): lax.dot_general(left_side, right_side, (((0,), (0,)), ((), ())), preferre...  53.2 us
    all_gather x2, waiting for transfers between devices, attn_gathered(): lax.all_gather(block, 'seq', axis=0, tiled=True)  51.1 us
    dot_general x5, matrix products, times_transposed(): lax.dot_general(left_side, right_side, (((1,), (1,)), ((), ())), preferre...  49 us
  transfers between devices with their start and end apart: 63, of which 19 were waited for; matrix products, arithmetic and copies ran while one was open for 49% of the time, Pallas kernels for 0%

profile of v2, /device:TPU:0, one launch (start us, length us, event | category | flops | bytes accessed | tf_op | source)
XLA Modules:
  0.0 1005.9 jit_solution(15475656206630718599)
XLA Ops:
  26.3 28.2 %all-gather.6.cloned.1.call-done = bf16[512,1664]{1,0:T(8,128)(2,1)} async-done(((bf16[128,1664]{1,0:T(8,128)(2,1)}), bf16[512,1664]{1,0:T(8,128)(2,1)}) %all-gather.6.cloned.1.call-update) | async-done | bytes 1703952 | tf_op jit(solution)/shard_map/all_gather | solution.py:170
  60.7 22.8 %all-gather.8.cloned.1.call-done = bf16[512,1024]{1,0:T(8,128)(2,1)} async-done(((bf16[128,1024]{1,0:T(8,128)(2,1)}), bf16[512,1024]{1,0:T(8,128)(2,1)}) %all-gather.8.cloned.1.call-update) | async-done | bytes 1048592 | tf_op jit(solution)/shard_map/all_gather | solution.py:170
  96.7 20.7 %collective-permute-done.7 = bf16[512,1024]{1,0:T(8,128)(2,1)} collective-permute-done((bf16[512,1024]{1,0:T(8,128)(2,1)}, bf16[512,1024]{1,0:T(8,128)(2,1)}, u32[]{:S(2)}, u32[]{:S(2)}) %collective-permute-start.7) | collective-permute-done | bytes 1048608 | tf_op jit(solution)/shard_map/ppermute | solution.py:82
  153.3 9.7 collective-permute-done.3
  164.0 33.2 %collective-permute-done.4 = bf16[256,512]{1,0:T(8,128)(2,1)} collective-permute-done((bf16[256,512]{1,0:T(8,128)(2,1)}, bf16[256,512]{1,0:T(8,128)(2,1)}, u32[]{:S(2)}, u32[]{:S(2)}) %collective-permute-start.4) | collective-permute-done | bytes 262176 | tf_op jit(solution)/shard_map/ppermute | solution.py:87
  275.8 31.5 %collective-permute-done.9 = bf16[512,2048]{1,0:T(8,128)(2,1)} collective-permute-done((bf16[512,2048]{1,0:T(8,128)(2,1)S(1)}, bf16[512,2048]{1,0:T(8,128)(2,1)}, u32[]{:S(2)}, u32[]{:S(2)}) %collective-permute-start.9) | collective-permute-done | bytes 2097184 | tf_op jit(solution)/shard_map/ppermute | solution.py:94
  329.9 33.4 %collective-permute-done.11 = bf16[512,2048]{1,0:T(8,128)(2,1)} collective-permute-done((bf16[512,2048]{1,0:T(8,128)(2,1)S(1)}, bf16[512,2048]{1,0:T(8,128)(2,1)}, u32[]{:S(2)}, u32[]{:S(2)}) %collective-permute-start.11) | collective-permute-done | bytes 2097184 | tf_op jit(solution)/shard_map/ppermute | solution.py:82
  365.0 41.8 %collective-permute-done.27 = bf16[512,2048]{1,0:T(8,128)(2,1)} collective-permute-done((bf16[512,2048]{1,0:T(8,128)(2,1)}, bf16[512,2048]{1,0:T(8,128)(2,1)}, u32[]{:S(2)}, u32[]{:S(2)}) %collective-permute-start.27) | collective-permute-done | bytes 2097184 | tf_op jit(solution)/shard_map/ppermute | solution.py:82
  406.8 15.8 %fusion.157 = f32[2048,1024]{1,0:T(8,128)} fusion(bf16[2048,1024]{0,1:T(8,128)(2,1)} %all-gather.12.cloned.1.call-done, bf16[512,2048]{1,0:T(8,128)(2,1)} %collective-permute-done.12, bf16[512,2048]{1,0:T(8,128)(2,1)} %collective-permute-done.11, bf16[512,2048]{1,0:T(8,128)(2,1)} %collective-permute-done.10, ...), kind=kOutput, calls=%fused_computation.484 | convolution fusion | flops 8623489024 | bytes 20971520 | tf_op jit(solution)/shard_map/dot_general | solution.py:331
  422.6 16.0 %fusion.158 = f32[2048,1024]{1,0:T(8,128)} fusion(bf16[2048,1024]{0,1:T(8,128)(2,1)} %all-gather.10.cloned.1.call-done, bf16[512,2048]{1,0:T(8,128)(2,1)} %collective-permute-done.12, bf16[512,2048]{1,0:T(8,128)(2,1)} %collective-permute-done.11, bf16[512,2048]{1,0:T(8,128)(2,1)} %collective-permute-done.10, ...), kind=kOutput, calls=%fused_computation.485 | convolution fusion | flops 8623489024 | bytes 20971520 | tf_op jit(solution)/shard_map/dot_general | solution.py:330
  442.9 22.9 %multiply_convert_fusion = (bf16[2048,1024]{1,0:T(8,128)(2,1)}, bf16[2048,1024]{1,0:T(8,128)(2,1)}, bf16[2048,1024]{1,0:T(8,128)(2,1)}) fusion(f32[2048,1024]{1,0:T(8,128)} %fusion.158, f32[2048,1024]{1,0:T(8,128)} %fusion.157, bf16[2048,1024]{0,1:T(8,128)(2,1)} %all-gather.14.cloned.1.call-done, bf16[512,2048]{1,0:T(8,128)(2,1)} %collective-permute-done.28, ...), kind=kOutput, calls=%fused_computation.43 | convolution fusion | flops 8654946304 | bytes 41943040 | tf_op jit(solution)/shard_map/dot_general | solution.py:341
  465.8 13.7 %convolution_convert_fusion.2 = bf16[2048,1024]{1,0:T(8,128)(2,1)} fusion(bf16[2048,1024]{1,0:T(8,128)(2,1)} %get-tuple-element.40, bf16[512,2048]{1,0:T(8,128)(2,1)} %collective-permute-done.12, bf16[512,2048]{1,0:T(8,128)(2,1)} %collective-permute-done.11, bf16[512,2048]{1,0:T(8,128)(2,1)} %collective-permute-done.10, ...), kind=kOutput, calls=%fused_computation.98 | convolution fusion | flops 8625586176 | bytes 16777216 | tf_op jit(solution)/shard_map/dot_general | solution.py:65
  479.6 15.5 %fusion.176 = f32[2048,2048]{1,0:T(8,128)} fusion(bf16[2048,1024]{1,0:T(8,128)(2,1)} %get-tuple-element.41, bf16[2048,1024]{0,1:T(8,128)(2,1)} %all-gather.10.cloned.1.call-done), kind=kOutput, calls=%fused_computation.499 | convolution fusion | flops 8589934592 | bytes 25165824 | tf_op jit(solution)/shard_map/dot_general | solution.py:59
  495.1 13.7 %add_convert_fusion = bf16[2048,2048]{1,0:T(8,128)(2,1)S(1)} fusion(f32[2048,2048]{1,0:T(8,128)} %fusion.176, bf16[2048,1024]{1,0:T(8,128)(2,1)} %get-tuple-element.40, bf16[2048,1024]{0,1:T(8,128)(2,1)S(1)} %copy-done.100), kind=kOutput, calls=%fused_computation | convolution fusion | flops 8598323200 | bytes 33554432 | tf_op jit(solution)/shard_map/dot_general | solution.py:59
  514.4 12.8 %convolution_convert_fusion.1 = bf16[2048,1024]{1,0:T(8,128)(2,1)} fusion(bf16[2048,1024]{1,0:T(8,128)(2,1)S(1)} %copy-done.103, bf16[512,2048]{1,0:T(8,128)(2,1)} %collective-permute-done.28, bf16[512,2048]{1,0:T(8,128)(2,1)} %collective-permute-done.27, bf16[512,2048]{1,0:T(8,128)(2,1)} %collective-permute-done.26, ...), kind=kOutput, calls=%fused_computation.97 | convolution fusion | flops 8625586176 | bytes 16777216 | tf_op jit(solution)/shard_map/dot_general | solution.py:65
  537.2 9.7 convolution_convert_fusion
  552.2 31.1 %collective-permute-done.31 = bf16[512,2048]{1,0:T(8,128)(2,1)S(1)} collective-permute-done((bf16[512,2048]{1,0:T(8,128)(2,1)S(1)}, bf16[512,2048]{1,0:T(8,128)(2,1)S(1)}, u32[]{:S(2)}, u32[]{:S(2)}) %collective-permute-start.31) | collective-permute-done | bytes 2097184 | tf_op jit(solution)/shard_map/ppermute | solution.py:82
  587.7 12.5 %convolution_convert_fusion.3 = bf16[2048,1024]{1,0:T(8,128)(2,1)} fusion(bf16[2048,1024]{1,0:T(8,128)(2,1)S(1)} %copy-done.102, bf16[512,2048]{1,0:T(8,128)(2,1)} %collective-permute-done.12, bf16[512,2048]{1,0:T(8,128)(2,1)} %collective-permute-done.11, bf16[512,2048]{1,0:T(8,128)(2,1)} %collective-permute-done.10, bf16[512,2048]{1,0:T(8,128)(2,1)S(1)} %copy-done.96), kind=kOutput, calls=%fused_computation.99 | convolution fusion | flops 8625586176 | bytes 16777216 | tf_op jit(solution)/shard_map/dot_general | solution.py:65
  600.3 32.8 %collective-permute-done.32 = bf16[512,2048]{1,0:T(8,128)(2,1)} collective-permute-done((bf16[512,2048]{1,0:T(8,128)(2,1)S(1)}, bf16[512,2048]{1,0:T(8,128)(2,1)}, u32[]{:S(2)}, u32[]{:S(2)}) %collective-permute-start.32) | collective-permute-done | bytes 2097184 | tf_op jit(solution)/shard_map/ppermute | solution.py:94
  695.4 10.9 %fusion.11 = bf16[4,512,1280]{1,2,0:T(8,128)(2,1)} fusion(f32[1280,512,4]{1,0,2:T(8,128)} %get-tuple-element.183, f32[4,512,1280]{1,2,0:T(8,128)} %get-tuple-element.175, f32[4,512]{1,0:T(4,128)S(1)} %get-tuple-element.182, f32[4,512]{1,0:T(4,128)S(1)} %log_add_fusion.3), kind=kLoop, calls=%fused_computation.20 | loop fusion | flops 10485760 | bytes 26230784 | tf_op jit(solution)/shard_map/convert_element_type | solution.py:78
  794.9 42.6 %collective-permute-done.24 = bf16[512,2048]{1,0:T(8,128)(2,1)S(1)} collective-permute-done((bf16[512,2048]{1,0:T(8,128)(2,1)S(1)}, bf16[512,2048]{1,0:T(8,128)(2,1)S(1)}, u32[]{:S(2)}, u32[]{:S(2)}) %collective-permute-start.24) | collective-permute-done | bytes 2097184 | tf_op jit(solution)/shard_map/ppermute | solution.py:82
  855.5 15.4 %collective-permute-done.39 = bf16[512,1536]{1,0:T(8,128)(2,1)} collective-permute-done((bf16[512,1536]{1,0:T(8,128)(2,1)}, bf16[512,1536]{1,0:T(8,128)(2,1)}, u32[]{:S(2)}, u32[]{:S(2)}) %collective-permute-start.39) | collective-permute-done | bytes 1572896 | tf_op jit(solution)/shard_map/ppermute | solution.py:82
  875.7 13.6 %collective-permute-done.25 = bf16[512,2048]{1,0:T(8,128)(2,1)} collective-permute-done((bf16[512,2048]{1,0:T(8,128)(2,1)}, bf16[512,2048]{1,0:T(8,128)(2,1)}, u32[]{:S(2)}, u32[]{:S(2)}) %collective-permute-start.25) | collective-permute-done | bytes 2097184 | tf_op jit(solution)/shard_map/ppermute | solution.py:94
  909.9 16.5 %collective-permute-done.49 = bf16[512,1024]{1,0:T(8,128)(2,1)S(1)} collective-permute-done((bf16[512,1024]{1,0:T(8,128)(2,1)S(1)}, bf16[512,1024]{1,0:T(8,128)(2,1)S(1)}, u32[]{:S(2)}, u32[]{:S(2)}) %collective-permute-start.49) | collective-permute-done | bytes 1048608 | tf_op jit(solution)/shard_map/ppermute | solution.py:82
  (616 shorter events, 472.1 us)
Async XLA Ops:
  12.5 71.1 %all-gather.8.cloned.1.call-start = ((), (), s32[]{:S(2)}) async-start(), calls=%async_computation.6 | async-start | bytes 1310720 | tf_op jit(solution)/shard_map/all_gather | solution.py:170
  15.4 79.5 %collective-permute-start.16 = (bf16[128,1024]{0,1:T(8,128)(2,1)}, bf16[128,1024]{0,1:T(8,128)(2,1)}, u32[]{:S(2)}, u32[]{:S(2)}) collective-permute-start(bf16[128,1024]{0,1:T(8,128)(2,1)} %get-tuple-element.157), channel_id=1, source_target_pairs={{0,24},{8,16},{16,8},{24,0},{1,25},{9,17},{17,9},{25,1},{2,26},{10... | collective-permute-start | bytes 786440 | tf_op jit(solution)/shard_map/ppermute | solution.py:82
  17.8 77.1 %collective-permute-start.17 = (bf16[128,1024]{0,1:T(8,128)(2,1)}, bf16[128,1024]{0,1:T(8,128)(2,1)}, u32[]{:S(2)}, u32[]{:S(2)}) collective-permute-start(bf16[128,1024]{0,1:T(8,128)(2,1)} %get-tuple-element.156), channel_id=1, source_target_pairs={{0,16},{8,24},{16,0},{24,8},{1,17},{9,25},{17,1},{25,9},{2,18},{10... | collective-permute-start | bytes 786440 | tf_op jit(solution)/shard_map/ppermute | solution.py:82
  18.4 77.2 %collective-permute-start.18 = (bf16[128,1024]{0,1:T(8,128)(2,1)}, bf16[128,1024]{0,1:T(8,128)(2,1)}, u32[]{:S(2)}, u32[]{:S(2)}) collective-permute-start(bf16[128,1024]{0,1:T(8,128)(2,1)} %get-tuple-element.155), channel_id=1, source_target_pairs={{0,8},{8,0},{16,24},{24,16},{1,9},{9,1},{17,25},{25,17},{2,10},{10... | collective-permute-start | bytes 786440 | tf_op jit(solution)/shard_map/ppermute | solution.py:82
  19.3 387.5 %all-gather.12.cloned.1.call-start = ((), (), s32[]{:S(2)}) async-start(), calls=%async_computation.8 | async-start | bytes 5242880 | tf_op jit(solution)/shard_map/all_gather | solution.py:195
  54.5 62.9 %collective-permute-start.1 = (bf16[512,1664]{1,0:T(8,128)(2,1)}, bf16[512,1664]{1,0:T(8,128)(2,1)}, u32[]{:S(2)}, u32[]{:S(2)}) collective-permute-start(bf16[512,1664]{1,0:T(8,128)(2,1)} %all-gather.6.cloned.1.call-done), channel_id=1, source_target_pairs={{0,16},{8,24},{16,0},{24,8},{1,17},{9,25},{17,1},{25,9},{2,18},{10... | collective-permute-start | bytes 5111816 | tf_op jit(solution)/shard_map/ppermute | solution.py:82
  94.9 176.8 %collective-permute-start.13 = (bf16[128,1024]{0,1:T(8,128)(2,1)}, bf16[128,1024]{0,1:T(8,128)(2,1)}, u32[]{:S(2)}, u32[]{:S(2)}) collective-permute-start(bf16[128,1024]{0,1:T(8,128)(2,1)} %get-tuple-element.151), channel_id=1, source_target_pairs={{0,24},{8,16},{16,8},{24,0},{1,25},{9,17},{17,9},{25,1},{2,26},{10... | collective-permute-start | bytes 786440 | tf_op jit(solution)/shard_map/ppermute | solution.py:82
  120.2 302.4 %all-gather.10.cloned.1.call-start = ((), (), s32[]{:S(2)}) async-start(), calls=%async_computation.7 | async-start | bytes 5242880 | tf_op jit(solution)/shard_map/all_gather | solution.py:195
  122.0 150.2 %collective-permute-start.14 = (bf16[128,1024]{0,1:T(8,128)(2,1)}, bf16[128,1024]{0,1:T(8,128)(2,1)}, u32[]{:S(2)}, u32[]{:S(2)}) collective-permute-start(bf16[128,1024]{0,1:T(8,128)(2,1)} %get-tuple-element.150), channel_id=1, source_target_pairs={{0,16},{8,24},{16,0},{24,8},{1,17},{9,25},{17,1},{25,9},{2,18},{10... | collective-permute-start | bytes 786440 | tf_op jit(solution)/shard_map/ppermute | solution.py:82
  163.0 109.3 %collective-permute-start.15 = (bf16[128,1024]{0,1:T(8,128)(2,1)}, bf16[128,1024]{0,1:T(8,128)(2,1)}, u32[]{:S(2)}, u32[]{:S(2)}) collective-permute-start(bf16[128,1024]{0,1:T(8,128)(2,1)} %get-tuple-element.149), channel_id=1, source_target_pairs={{0,8},{8,0},{16,24},{24,16},{1,9},{9,1},{17,25},{25,17},{2,10},{10... | collective-permute-start | bytes 786440 | tf_op jit(solution)/shard_map/ppermute | solution.py:82
  197.2 130.5 %collective-permute-start.19 = (bf16[128,1024]{0,1:T(8,128)(2,1)}, bf16[128,1024]{0,1:T(8,128)(2,1)}, u32[]{:S(2)}, u32[]{:S(2)}) collective-permute-start(bf16[128,1024]{0,1:T(8,128)(2,1)} %get-tuple-element.145), channel_id=1, source_target_pairs={{0,24},{8,16},{16,8},{24,0},{1,25},{9,17},{17,9},{25,1},{2,26},{10... | collective-permute-start | bytes 786440 | tf_op jit(solution)/shard_map/ppermute | solution.py:82
  275.7 167.2 %all-gather.14.cloned.1.call-start = ((), (), s32[]{:S(2)}) async-start(), calls=%async_computation.9 | async-start | bytes 5242880 | tf_op jit(solution)/shard_map/all_gather | solution.py:195
  326.5 80.3 %collective-permute-start.27 = (bf16[512,2048]{1,0:T(8,128)(2,1)}, bf16[512,2048]{1,0:T(8,128)(2,1)}, u32[]{:S(2)}, u32[]{:S(2)}) collective-permute-start(bf16[512,2048]{1,0:T(8,128)(2,1)} %slice_dynamic-update-slice_fusion.16), channel_id=1, source_target_pairs={{0,16},{8,24},{16,0},{24,8},{1,17},{9,25},{17,1},{25,9},{2,18},{10... | collective-permute-start | bytes 6291464 | tf_op jit(solution)/shard_map/ppermute | solution.py:82
  329.8 77.0 %collective-permute-start.10 = (bf16[512,2048]{1,0:T(8,128)(2,1)S(1)}, bf16[512,2048]{1,0:T(8,128)(2,1)}, u32[]{:S(2)}, u32[]{:S(2)}) collective-permute-start(bf16[512,2048]{1,0:T(8,128)(2,1)S(1)} %slice_dynamic-update-slice_fusion), channel_id=1, source_target_pairs={{0,8},{8,0},{16,24},{24,16},{1,9},{9,1},{17,25},{25,17},{2,10},{10... | collective-permute-start | bytes 6291464 | tf_op jit(solution)/shard_map/ppermute | solution.py:82
  364.4 563.6 %reduce-scatter.10.cloned.1.call-start = ((), (), s32[]{:S(2)}) async-start(), calls=%async_computation.12 | async-start | bytes 5242880 | tf_op jit(solution)/shard_map/reduce_scatter | solution.py:200
  364.4 74.1 %collective-permute-start.26 = (bf16[512,2048]{1,0:T(8,128)(2,1)}, bf16[512,2048]{1,0:T(8,128)(2,1)}, u32[]{:S(2)}, u32[]{:S(2)}) collective-permute-start(bf16[512,2048]{1,0:T(8,128)(2,1)} %slice_dynamic-update-slice_fusion.16), channel_id=1, source_target_pairs={{0,8},{8,0},{16,24},{24,16},{1,9},{9,1},{17,25},{25,17},{2,10},{10... | collective-permute-start | bytes 6291464 | tf_op jit(solution)/shard_map/ppermute | solution.py:82
  479.5 454.9 %reduce-scatter.14.cloned.1.call-start = ((), (), s32[]{:S(2)}) async-start(), calls=%async_computation.14 | async-start | bytes 5242880 | tf_op jit(solution)/shard_map/reduce_scatter | solution.py:200
  527.4 416.7 %reduce-scatter.8.cloned.1.call-start = ((), (), s32[]{:S(2)}) async-start(), calls=%async_computation.11 | async-start | bytes 5242880 | tf_op jit(solution)/shard_map/reduce_scatter | solution.py:200
  551.6 234.3 %collective-permute-start.23 = (bf16[512,2048]{1,0:T(8,128)(2,1)}, bf16[512,2048]{1,0:T(8,128)(2,1)}, u32[]{:S(2)}, u32[]{:S(2)}) collective-permute-start(bf16[512,2048]{1,0:T(8,128)(2,1)} %get-tuple-element.46), channel_id=1, source_target_pairs={{0,8},{8,0},{16,24},{24,16},{1,9},{9,1},{17,25},{25,17},{2,10},{10... | collective-permute-start | bytes 6291464 | tf_op jit(solution)/shard_map/ppermute | solution.py:82
  551.7 243.2 %collective-permute-start.22 = (bf16[512,2048]{1,0:T(8,128)(2,1)}, bf16[512,2048]{1,0:T(8,128)(2,1)}, u32[]{:S(2)}, u32[]{:S(2)}) collective-permute-start(bf16[512,2048]{1,0:T(8,128)(2,1)} %get-tuple-element.45), channel_id=1, source_target_pairs={{0,8},{8,0},{16,24},{24,16},{1,9},{9,1},{17,25},{25,17},{2,10},{10... | collective-permute-start | bytes 6291464 | tf_op jit(solution)/shard_map/ppermute | solution.py:82
  600.2 382.1 %reduce-scatter.6.cloned.1.call-start = ((), (), s32[]{:S(2)}) async-start(), calls=%async_computation.10 | async-start | bytes 1966080 | tf_op jit(solution)/shard_map/reduce_scatter | solution.py:183
  790.5 65.0 %collective-permute-start.37 = (bf16[512,1536]{1,0:T(8,128)(2,1)}, bf16[512,1536]{1,0:T(8,128)(2,1)}, u32[]{:S(2)}, u32[]{:S(2)}) collective-permute-start(bf16[512,1536]{1,0:T(8,128)(2,1)} %get-tuple-element.47), channel_id=1, source_target_pairs={{0,8},{8,0},{16,24},{24,16},{1,9},{9,1},{17,25},{25,17},{2,10},{10... | collective-permute-start | bytes 4718600 | tf_op jit(solution)/shard_map/ppermute | solution.py:82
  794.3 76.6 %collective-permute-start.39 = (bf16[512,1536]{1,0:T(8,128)(2,1)}, bf16[512,1536]{1,0:T(8,128)(2,1)}, u32[]{:S(2)}, u32[]{:S(2)}) collective-permute-start(bf16[512,1536]{1,0:T(8,128)(2,1)} %fusion.52), channel_id=1, source_target_pairs={{0,16},{8,24},{16,0},{24,8},{1,17},{9,25},{17,1},{25,9},{2,18},{10... | collective-permute-start | bytes 4718600 | tf_op jit(solution)/shard_map/ppermute | solution.py:82
  875.5 121.0 %reduce-scatter.12.cloned.1.call-start = ((), (), s32[]{:S(2)}) async-start(), calls=%async_computation.13 | async-start | bytes 1310720 | tf_op jit(solution)/shard_map/reduce_scatter | solution.py:183
  (164 other events, 3520.7 us)
Sparse Core Ops, SparseCore 0:
  12.6 41.8 all-gather.5
  56.7 26.8 all-gather.7
  120.3 101.7 all-gather.11
  275.9 78.2 all-gather.9
  364.5 78.3 all-gather.13
  479.7 75.2 reduce-scatter.9
  557.3 77.2 reduce-scatter.13
  636.9 77.2 reduce-scatter.7
  875.6 38.4 reduce-scatter.5
  928.1 29.4 reduce-scatter.11
